TPU v7x, 32 devices: a whole 2x2x4 slice. The times are simulated.
32 devices in a mesh: gx: 4 (over y, core), gy: 2 (over x), af: 4 (over z).
Axes of the slice: x: 2, y: 2, z: 4, core: 2. Of those that a mesh axis runs over, the one named last changes fastest.
Arguments:
- volume: bfloat16 [32, 16, 32, 128], P('af', 'gx', 'gy'), may hold values from -6 to 6
- weight_one: bfloat16 [32, 32, 3, 3, 3], P('af'), may hold values from -0.21875 to 0.21875
- bias_one: float32 [32], P('af'), may hold values from -1 to 1
- weight_two: bfloat16 [32, 32, 3, 3, 3], P('af'), may hold values from -0.21875 to 0.21875
- cotangent: bfloat16 [32, 16, 32, 128], P('af', 'gx', 'gy'), may hold values from -6 to 6
Outputs:
- output: bfloat16 [32, 16, 32, 128], P('af', 'gx', 'gy')
- input_grad: bfloat16 [32, 16, 32, 128], P('af', 'gx', 'gy')
- grad_one: float32 [32, 32, 3, 3, 3], P('af')
- bias_grad: float32 [32], P('af')
- grad_two: float32 [32, 32, 3, 3, 3], P('af')
All inputs are finite; a program needn't handle non-finite values.
Results may differ from a plain program's by a relative error of at most 0.0065.
Values may be sent and summed in bfloat16 or wider, within the bound.
No kernel may reach another device: no remote copies, remote signals or barrier semaphores. Data moves between devices by JAX's collectives and lax.ppermute only.
A program may use at most 64 MiB of HBM per device.

v0:
```python
import functools
import math

import jax
import jax.numpy as jnp
from jax import lax
from jax.experimental import pallas as pl
from jax.experimental.pallas import tpu as pltpu
from jax.sharding import PartitionSpec as P

BF = jnp.bfloat16
F32 = jnp.float32
ALL = ("gx", "gy", "af")
RIM = 2


def place(sizes):
    me = lax.axis_index("af")
    row = lax.axis_index("gy")
    part = part_of(me, row, sizes)
    return me, row, part, row * sizes["af"] + part


def part_of(chan, row, sizes):
    return jnp.where(row % 2 == 0, chan, sizes["af"] - 1 - chan)


def own_order(parts, me):
    bit = 1
    while bit < len(parts):
        turn = (me & bit) != 0
        parts = [lax.select(turn, parts[g ^ bit], parts[g]) for g in range(len(parts))]
        bit *= 2
    return parts


def pack_body(sizes, vol_ref, cot_ref, *refs):
    groups = sizes["af"]
    outs, (flat, turned) = refs[:groups], refs[groups:]
    chans, nx, ny, nz = vol_ref.shape
    rows = ny // groups
    me, row, _, _ = place(sizes)
    for a, ref in enumerate((vol_ref, cot_ref)):
        for x in range(nx):
            flat[a, x] = ref[:, x].astype(F32).reshape(chans * ny, nz)
    for a in range(2):
        for x in range(nx):
            for y in range(ny):
                turned[y, a, x] = flat[a, x, pl.ds(y, chans, stride=ny), :].astype(BF)
    for s in range(groups):
        start = part_of(me ^ s, row, sizes) * rows
        for r in range(rows):
            outs[s][r] = turned[start + r]


def join_body(sizes, *refs):
    groups = sizes["af"]
    parts, (core_ref, first_ref, second_ref) = refs[:groups], refs[groups:]
    rows, fields, nx = parts[0].shape[:3]
    me, _, _, spot = place(sizes)
    even = spot % 2 == 0
    for a in range(fields):
        for x in range(nx):
            tiles = []
            for y in range(rows):
                cells = own_order([p[y, a, x].astype(F32) for p in parts], me)
                tiles.append(jnp.concatenate(cells, axis=0))
                core_ref[a, x, y] = tiles[-1].astype(BF)
            for h in range(RIM):
                head, tail = tiles[h], tiles[rows - RIM + h]
                first_ref[a, x, h] = lax.select(even, tail, head).astype(BF)
                second_ref[a, x, h] = lax.select(even, head, tail).astype(BF)


def y_rim(sizes, ya, yb, idx, h, spot, upper):
    even = spot % 2 == 0
    spots = sizes["gy"] * sizes["af"]
    first, second = ya[idx + (h,)].astype(F32), yb[idx + (h,)].astype(F32)
    if upper:
        got, inside = lax.select(even, first, second), spot < spots - 1
    else:
        got, inside = lax.select(even, second, first), spot > 0
    return lax.select(inside, got, jnp.zeros_like(got))


def edge_body(sizes, core, ya, yb, first_ref, second_ref):
    fields, nx, rows = core.shape[:3]
    spot = place(sizes)[3]
    even = lax.axis_index("gx") % 2 == 0
    for ref, from_tail in ((first_ref, even), (second_ref, jnp.logical_not(even))):
        start = jnp.where(from_tail, nx - RIM, 0)
        for a in range(fields):
            for h in range(RIM):
                x = start + h
                for r in range(RIM):
                    ref[a, h, r] = y_rim(sizes, ya, yb, (a, x), r, spot, False).astype(BF)
                    ref[a, h, RIM + rows + r] = y_rim(
                        sizes, ya, yb, (a, x), r, spot, True
                    ).astype(BF)
                for y in range(rows):
                    ref[a, h, RIM + y] = core[a, x, y]


def weight_pack_body(one_ref, two_ref, bias_ref, out_ref):
    taps, chans, width = one_ref.shape
    per = 128 // width
    tiles = out_ref.shape[1]
    sub = lax.broadcasted_iota(jnp.int32, (chans, width), 0)
    lane = lax.broadcasted_iota(jnp.int32, (chans, width), 1)
    bias = jnp.zeros((chans, width), F32)
    for c in range(chans):
        bias = jnp.where(sub == c, bias_ref[c], bias)
    top = bias.astype(BF).astype(F32)
    mid = (bias - top).astype(BF).astype(F32)
    low = bias - top - mid
    extra = jnp.where(lane == 0, top, jnp.where(lane == 1, mid, jnp.where(lane == 2, low, 0.0)))
    none = jnp.zeros_like(extra)
    for k, ref in enumerate((one_ref, two_ref)):
        for t in range(tiles):
            cells = []
            for j in range(per):
                tap = t * per + j
                if tap < taps:
                    cells.append(ref[tap].astype(F32))
                else:
                    cells.append(extra if k == 0 and tap == taps else none)
            out_ref[k, t] = jnp.concatenate(cells, axis=1).astype(BF)


def weight_join_body(sizes, taps, *refs):
    groups = sizes["af"]
    parts, outs = refs[:groups], refs[groups:]
    kinds, tiles, chans = parts[0].shape[:3]
    width = chans * groups
    per = 128 // width
    me = lax.axis_index("af")
    for k in range(kinds):
        plain, turned = outs[2 * k], outs[2 * k + 1]
        blocks = {}
        for t in range(tiles):
            cells = own_order([p[k, t].astype(F32) for p in parts], me)
            tile = jnp.concatenate(cells, axis=0)
            plain[:, t * 128 : (t + 1) * 128] = tile.astype(BF)
            back = tile.T
            for j in range(per):
                blocks[t * per + j] = back[j * width : (j + 1) * width]
        none = jnp.zeros((width, width), F32)
        for t in range(tiles):
            cells = []
            for j in range(per):
                tap = t * per + j
                cells.append(blocks[taps - 1 - tap] if tap < taps else none)
            turned[:, t * 128 : (t + 1) * 128] = jnp.concatenate(cells, axis=1).astype(BF)


def spread(ref, x, y, tile):
    nz = tile.shape[1]
    lane = lax.broadcasted_iota(jnp.int32, tile.shape, 1)
    below = jnp.where(lane == 0, 0.0, pltpu.roll(tile, 1, 1))
    above = jnp.where(lane == nz - 1, 0.0, pltpu.roll(tile, nz - 1, 1))
    ref[x, y] = jnp.concatenate([below, tile, above], axis=0).astype(BF)


def extra_rows(width, count):
    sub = lax.broadcasted_iota(jnp.int32, (width, count), 0)
    return jnp.where(sub < 3, 1.0, 0.0).astype(BF)


def window(ref, x, ys, extra):
    columns = []
    for y in ys:
        pieces = [ref[x + i, y + j] for i in range(3) for j in range(3)]
        columns.append(jnp.concatenate(pieces + [extra], axis=0))
    return jnp.concatenate(columns, axis=1) if len(columns) > 1 else columns[0]


def dot(left, right):
    return lax.dot_general(left, right, (((1,), (0,)), ((), ())), preferred_element_type=F32)


def dot_cells(left, right):
    return lax.dot_general(left, right, (((1,), (1,)), ((), ())), preferred_element_type=F32)


def fields_body(sizes, core, ya, yb, xa, xb, one_ref, two_ref, *refs):
    groups = sizes["af"]
    hid_ref, pre_ref = refs[:2]
    outs = refs[2 : 2 + groups]
    vol_s, cot_s, hid_s, pre_s, acc = refs[2 + groups :]
    _, nx, rows, width, nz = core.shape
    me, _, _, spot = place(sizes)
    gx = lax.axis_index("gx")
    even = gx % 2 == 0
    spots = sizes["gy"] * groups
    inside_low, inside_high = gx > 0, gx < sizes["gx"] - 1
    extra = extra_rows(width, nz)

    for a, ref in enumerate((vol_s, cot_s)):

        def middle(x, carry):
            for y in range(rows):
                spread(ref, RIM + x, RIM + y, core[a, x, y].astype(F32))
            for h in range(RIM):
                spread(ref, RIM + x, h, y_rim(sizes, ya, yb, (a, x), h, spot, False))
                spread(
                    ref, RIM + x, RIM + rows + h, y_rim(sizes, ya, yb, (a, x), h, spot, True)
                )
            return carry

        lax.fori_loop(0, nx, middle, 0)

        def sides(h, carry):
            for y in range(rows + 2 * RIM):
                first, second = xa[a, h, y].astype(F32), xb[a, h, y].astype(F32)
                none = jnp.zeros_like(first)
                low = lax.select(even, second, first)
                high = lax.select(even, first, second)
                spread(ref, h, y, lax.select(inside_low, low, none))
                spread(ref, RIM + nx + h, y, lax.select(inside_high, high, none))
            return carry

        lax.fori_loop(0, RIM, sides, 0)

    def field_row(x, carry):
        x_in = jnp.logical_and(
            jnp.logical_or(x > 0, inside_low), jnp.logical_or(x < nx + 1, inside_high)
        )
        for start in range(0, rows + 2, 2):
            ys = list(range(start, min(start + 2, rows + 2)))
            pre_act = dot(one_ref[...], window(vol_s, x, ys, extra))
            hid_grad = dot(two_ref[...], window(cot_s, x, ys, extra))
            sigma = 1.0 / (1.0 + jnp.exp(-pre_act))
            hidden = pre_act * sigma
            pre_grad = hid_grad * sigma * (1.0 + pre_act * (1.0 - sigma))
            for n, y in enumerate(ys):
                ok = x_in
                if y == 0:
                    ok = jnp.logical_and(ok, spot > 0)
                if y == rows + 1:
                    ok = jnp.logical_and(ok, spot < spots - 1)
                for full, out, stack in ((hidden, hid_ref, hid_s), (pre_grad, pre_ref, pre_s)):
                    tile = full[:, n * nz : (n + 1) * nz]
                    tile = lax.select(ok, tile, jnp.zeros_like(tile)).astype(BF)
                    out[x, y] = tile
                    spread(stack, x, y, tile.astype(F32))
        return carry

    lax.fori_loop(0, nx + 2, field_row, 0)

    acc[...] = jnp.zeros_like(acc)

    def grad_row(x, carry):
        ys = list(range(rows))
        cot = [cot_s[RIM + x, RIM + y, width : 2 * width] for y in ys]
        acc[0] += dot_cells(jnp.concatenate(cot, axis=1), window(hid_s, x, ys, extra))
        pre = [pre_s[1 + x, 1 + y, width : 2 * width] for y in ys]
        acc[1] += dot_cells(
            jnp.concatenate(pre, axis=1), window(vol_s, x + 1, [y + 1 for y in ys], extra)
        )
        return carry

    lax.fori_loop(0, nx, grad_row, 0)

    chans = width // groups
    for s in range(groups):
        start = pl.multiple_of((me ^ s) * chans, chans)
        for k in range(2):
            outs[s][k] = acc[k, pl.ds(start, chans), :]


def outputs_body(sizes, hid_ref, pre_ref, two_ref, one_ref, *refs):
    groups = sizes["af"]
    outs, (hid_s, pre_s, turned) = refs[:groups], refs[groups:]
    nx, rows, width, nz = hid_ref.shape
    nx, rows = nx - 2, rows - 2
    chans = width // groups
    me = lax.axis_index("af")
    extra = jnp.zeros((width, nz), BF)

    def fill(x, carry):
        for y in range(rows + 2):
            spread(hid_s, x, y, hid_ref[x, y].astype(F32))
            spread(pre_s, x, y, pre_ref[x, y].astype(F32))
        return carry

    lax.fori_loop(0, nx + 2, fill, 0)

    def out_row(x, carry):
        for start in range(0, rows, 2):
            ys = list(range(start, min(start + 2, rows)))
            for a, (ref, stack) in enumerate(((two_ref, hid_s), (one_ref, pre_s))):
                got = dot(ref[...], window(stack, x, ys, extra))
                for n, y in enumerate(ys):
                    for g in range(groups):
                        turned[g, y, a, x] = got[
                            g * chans : (g + 1) * chans, n * nz : (n + 1) * nz
                        ].astype(BF)
        return carry

    lax.fori_loop(0, nx, out_row, 0)
    for s in range(groups):
        outs[s][...] = turned[me ^ s]


def unpack_body(sizes, *refs):
    groups = sizes["af"]
    parts, (out_ref, grad_ref, flat) = refs[:groups], refs[groups:]
    rows, _, nx, chans, nz = parts[0].shape
    ny = rows * groups
    me, row, _, _ = place(sizes)
    for s in range(groups):
        start = part_of(me ^ s, row, sizes) * rows
        for y in range(rows):
            for a in range(2):
                for x in range(nx):
                    spot = pl.multiple_of((start + y) * chans, chans)
                    flat[a, x, pl.ds(spot, chans), :] = parts[s][y, a, x].astype(F32)
    for a, ref in enumerate((out_ref, grad_ref)):
        for x in range(nx):
            for c in range(chans):
                ref[c, x] = flat[a, x, pl.ds(c, ny, stride=chans), :].astype(BF)


def total_body(scale, taps, width, own_ref, got_ref, one_ref, two_ref, bias_ref):
    per = 128 // width
    for k, ref in ((1, one_ref), (0, two_ref)):
        total = (own_ref[k] + got_ref[k]) * scale
        for tap in range(taps):
            ref[tap] = total[:, tap * width : (tap + 1) * width]
        if k == 1:
            bias_ref[...] = total[:, taps * width : taps * width + 1]


def call(body, outs, scratch, args, specs=None, flops=0):
    moved = sum(math.prod(a.shape) * a.dtype.itemsize for a in args)
    moved += sum(math.prod(o.shape) * o.dtype.itemsize for o in outs)
    return pl.pallas_call(
        body,
        out_shape=tuple(outs),
        in_specs=specs or [pl.BlockSpec(memory_space=pltpu.VMEM)] * len(args),
        out_specs=tuple(pl.BlockSpec(memory_space=pltpu.VMEM) for _ in outs),
        scratch_shapes=scratch,
        cost_estimate=pl.CostEstimate(flops=flops, bytes_accessed=moved, transcendentals=0),
    )(*args)


def swap(value, axes, pairs):
    return lax.ppermute(value, axes, pairs)


def across(value, step, sizes):
    return swap(value, "af", [(i, i ^ step) for i in range(sizes["af"])])


def ring_pairs(count, second):
    if not second:
        return [(i, i ^ 1) for i in range(count)]
    return [(i, ((((i - 1) % count) ^ 1) + 1) % count) for i in range(count)]


def y_pairs(sizes, second):
    groups = sizes["af"]

    def spot(i):
        row, part = divmod(i, groups)
        return row * groups + (part if row % 2 == 0 else groups - 1 - part)

    pairs = ring_pairs(sizes["gy"] * groups, second)
    return [(spot(i), spot(j)) for i, j in pairs]


def body(sizes, volume, weight_one, bias_one, weight_two, cotangent):
    groups = sizes["af"]
    chans, nx, ny, nz = volume.shape
    width = chans * groups
    rows = ny // groups
    taps = 27
    tiles = -(-(taps + 1) * width // 128)
    columns = tiles * 128
    bind = functools.partial
    shape = jax.ShapeDtypeStruct

    piece = shape((rows, 2, nx, chans, nz), BF)
    sent = call(
        bind(pack_body, sizes),
        [piece] * groups,
        [pltpu.VMEM((2, nx, chans * ny, nz), F32), pltpu.VMEM((ny, 2, nx, chans, nz), BF)],
        (volume, cotangent),
    )
    parts = [sent[0]] + [across(sent[s], s, sizes) for s in range(1, groups)]

    rim = shape((2, nx, RIM, width, nz), BF)
    core, first, second = call(
        bind(join_body, sizes), [shape((2, nx, rows, width, nz), BF), rim, rim], [], parts
    )
    ya = swap(first, ("gy", "af"), y_pairs(sizes, False))
    yb = swap(second, ("gy", "af"), y_pairs(sizes, True))

    taps_first = [jnp.transpose(w, (2, 3, 4, 0, 1)).reshape(taps, chans, width) for w in (weight_one, weight_two)]
    vmem = pl.BlockSpec(memory_space=pltpu.VMEM)
    (own_w,) = call(
        weight_pack_body,
        [shape((2, tiles, chans, 128), BF)],
        [],
        (*taps_first, bias_one),
        [vmem, vmem, pl.BlockSpec(memory_space=pltpu.SMEM)],
    )

    side = shape((2, RIM, rows + 2 * RIM, width, nz), BF)
    first, second = call(bind(edge_body, sizes), [side, side], [], (core, ya, yb))
    xa = swap(first, "gx", ring_pairs(sizes["gx"], False))
    xb = swap(second, "gx", ring_pairs(sizes["gx"], True))

    weights = [own_w] + [across(own_w, s, sizes) for s in range(1, groups)]
    flat_w = shape((width, columns), BF)
    one, one_t, two, two_t = call(
        bind(weight_join_body, sizes, taps), [flat_w] * 4, [], weights
    )

    field = shape((nx + 2, rows + 2, width, nz), BF)
    share = shape((2, chans, columns), F32)
    got = call(
        bind(fields_body, sizes),
        [field, field] + [share] * groups,
        [
            pltpu.VMEM((nx + 4, rows + 4, 3 * width, nz), BF),
            pltpu.VMEM((nx + 4, rows + 4, 3 * width, nz), BF),
            pltpu.VMEM((nx + 2, rows + 2, 3 * width, nz), BF),
            pltpu.VMEM((nx + 2, rows + 2, 3 * width, nz), BF),
            pltpu.VMEM((2, width, columns), F32),
        ],
        (core, ya, yb, xa, xb, one, two_t),
        flops=4 * width * columns * nz * ((nx + 2) * (rows + 2) + nx * rows),
    )
    hidden, pre_grad, shares = got[0], got[1], got[2:]

    total = shares[0]
    for s in range(1, groups):
        total = total + across(shares[s], s, sizes)
    steps = []
    for axis in ("gy", "gx"):
        bit = 1
        while bit < sizes[axis]:
            steps.append((axis, [(i, i ^ bit) for i in range(sizes[axis])]))
            bit *= 2
    for axis, pairs in steps[:-1]:
        total = total + swap(total, axis, pairs)
    last = swap(total, *steps[-1])

    pieces = call(
        bind(outputs_body, sizes),
        [piece] * groups,
        [
            pltpu.VMEM((nx + 2, rows + 2, 3 * width, nz), BF),
            pltpu.VMEM((nx + 2, rows + 2, 3 * width, nz), BF),
            pltpu.VMEM((groups, rows, 2, nx, chans, nz), BF),
        ],
        (hidden, pre_grad, two, one_t),
        flops=4 * width * columns * nz * nx * rows,
    )
    pieces = [pieces[0]] + [across(pieces[s], s, sizes) for s in range(1, groups)]
    block = shape((chans, nx, ny, nz), BF)
    output, input_grad = call(
        bind(unpack_body, sizes),
        [block, block],
        [pltpu.VMEM((2, nx, chans * ny, nz), F32)],
        pieces,
    )

    cells = nx * sizes["gx"] * ny * sizes["gy"] * nz
    tap_grad = shape((taps, chans, width), F32)
    grad_one, grad_two, bias_grad = call(
        bind(total_body, 1.0 / math.sqrt(cells), taps, width),
        [tap_grad, tap_grad, shape((chans, 1), F32)],
        [],
        (total, last),
    )

    def unturn(grad):
        return jnp.transpose(grad.reshape(3, 3, 3, chans, width), (3, 4, 0, 1, 2))

    return output, input_grad, unturn(grad_one), bias_grad.reshape(chans), unturn(grad_two)


def solution(mesh):
    return jax.shard_map(
        functools.partial(body, dict(mesh.shape)),
        mesh=mesh,
        in_specs=(
            P("af", "gx", "gy", None),
            P("af", None, None, None, None),
            P("af"),
            P("af", None, None, None, None),
            P("af", "gx", "gy", None),
        ),
        out_specs=(
            P("af", "gx", "gy", None),
            P("af", "gx", "gy", None),
            P("af", None, None, None, None),
            P("af"),
            P("af", None, None, None, None),
        ),
        check_vma=False,
    )
```

profile of v0, /device:TPU:0, one launch (start us, length us, event | category | flops | bytes accessed | tf_op | source)
XLA Modules:
  0.0 82.0 jit_solution(16100915810309263406)
XLA Ops:
  0.6 1.9 %shard_map.92 = (bf16[4,2,4,8,128]{4,3,2,1,0:T(8,128)(2,1)}, bf16[4,2,4,8,128]{4,3,2,1,0:T(8,128)(2,1)}, bf16[4,2,4,8,128]{4,3,2,1,0:T(8,128)(2,1)}, bf16[4,2,4,8,128]{4,3,2,1,0:T(8,128)(2,1)}) custom-call(bf16[8,4,16,128]{3,2,1,0:T(8,128)(2,1)} %vol_ref.1, bf16[8,4,16,128]{3,2,1,0:T(8,128)(2,1)} %cot_ref.1), custom_call_target="tpu_custom_call" | custom-call | bytes 524288 | tf_op jit(solution)/shard_map/pallas_call | solution.py:337
  2.5 3.1 %collective-permute-start = (bf16[4,2,4,8,128]{4,3,2,1,0:T(8,128)(2,1)}, bf16[4,2,4,8,128]{4,3,2,1,0:T(8,128)(2,1)S(1)}, u32[]{:S(2)}, u32[]{:S(2)}) collective-permute-start(bf16[4,2,4,8,128]{4,3,2,1,0:T(8,128)(2,1)} %get-tuple-element.34), channel_id=1, source_target_pairs={{0,1},{1,0},{2,3},{3,2},{4,5},{5,4},{6,7},{7,6},{8,9},{9,8},{10,11... | collective-permute-start | bytes 196616 | tf_op jit(solution)/shard_map/ppermute | solution.py:348
  5.5 2.6 %collective-permute-start.1 = (bf16[4,2,4,8,128]{4,3,2,1,0:T(8,128)(2,1)}, bf16[4,2,4,8,128]{4,3,2,1,0:T(8,128)(2,1)S(1)}, u32[]{:S(2)}, u32[]{:S(2)}) collective-permute-start(bf16[4,2,4,8,128]{4,3,2,1,0:T(8,128)(2,1)} %get-tuple-element.35), channel_id=1, source_target_pairs={{0,2},{1,3},{2,0},{3,1},{4,6},{5,7},{6,4},{7,5},{8,10},{9,11},{10,... | collective-permute-start | bytes 196616 | tf_op jit(solution)/shard_map/ppermute | solution.py:348
  8.1 4.9 %collective-permute-done.1.refs_2_ = bf16[4,2,4,8,128]{4,3,2,1,0:T(8,128)(2,1)S(1)} collective-permute-done((bf16[4,2,4,8,128]{4,3,2,1,0:T(8,128)(2,1)}, bf16[4,2,4,8,128]{4,3,2,1,0:T(8,128)(2,1)S(1)}, u32[]{:S(2)}, u32[]{:S(2)}) %collective-permute-start.1) | collective-permute-done | bytes 65568 | tf_op jit(solution)/shard_map/ppermute | solution.py:348
  15.0 1.8 %shard_map.93 = (bf16[2,4,4,32,128]{4,3,2,1,0:T(8,128)(2,1)}, bf16[2,4,2,32,128]{4,3,2,1,0:T(8,128)(2,1)}, bf16[2,4,2,32,128]{4,3,2,1,0:T(8,128)(2,1)}) custom-call(bf16[4,2,4,8,128]{4,3,2,1,0:T(8,128)(2,1)} %get-tuple-element.33.refs_0_, bf16[4,2,4,8,128]{4,3,2,1,0:T(8,128)(2,1)} %copy-done.6, bf16[4,2,4,8,128]{4,3,2,1,0:T(8,128)(2,1)} %copy-done.7, ...), custom_call_target="tpu_custom_call" | custom-call | bytes 786432 | tf_op jit(solution)/shard_map/pallas_call | solution.py:337
  18.3 3.7 %collective-permute-done.3.ya = bf16[2,4,2,32,128]{4,3,2,1,0:T(8,128)(2,1)S(1)} collective-permute-done((bf16[2,4,2,32,128]{4,3,2,1,0:T(8,128)(2,1)}, bf16[2,4,2,32,128]{4,3,2,1,0:T(8,128)(2,1)S(1)}, u32[]{:S(2)}, u32[]{:S(2)}) %collective-permute-start.3) | collective-permute-done | bytes 131104 | tf_op jit(solution)/shard_map/ppermute | solution.py:348
  22.7 1.9 %shard_map.94 = (bf16[2,2,8,32,128]{4,3,2,1,0:T(8,128)(2,1)}, bf16[2,2,8,32,128]{4,3,2,1,0:T(8,128)(2,1)}) custom-call(bf16[2,4,4,32,128]{4,3,2,1,0:T(8,128)(2,1)} %get-tuple-element.37.core, bf16[2,4,2,32,128]{4,3,2,1,0:T(8,128)(2,1)} %copy-done.1, bf16[2,4,2,32,128]{4,3,2,1,0:T(8,128)(2,1)} %copy-done.2), custom_call_target="tpu_custom_call" | custom-call | bytes 1048576 | tf_op jit(solution)/shard_map/pallas_call | solution.py:337
  24.6 1.6 %collective-permute-start.6 = (bf16[2,2,8,32,128]{4,3,2,1,0:T(8,128)(2,1)}, bf16[2,2,8,32,128]{4,3,2,1,0:T(8,128)(2,1)S(1)}, u32[]{:S(2)}, u32[]{:S(2)}) collective-permute-start(bf16[2,2,8,32,128]{4,3,2,1,0:T(8,128)(2,1)} %get-tuple-element.41), channel_id=1, source_target_pairs={{0,24},{8,16},{16,8},{24,0},{1,25},{9,17},{17,9},{25,1},{2,26},{10... | collective-permute-start | bytes 786440 | tf_op jit(solution)/shard_map/ppermute | solution.py:348
  27.8 3.0 %collective-permute-start.9 = (bf16[2,7,8,128]{3,2,1,0:T(8,128)(2,1)}, bf16[2,7,8,128]{3,2,1,0:T(8,128)(2,1)S(1)}, u32[]{:S(2)}, u32[]{:S(2)}) collective-permute-start(bf16[2,7,8,128]{3,2,1,0:T(8,128)(2,1)} %shard_map.95.refs_0_), channel_id=1, source_target_pairs={{0,3},{1,2},{2,1},{3,0},{4,7},{5,6},{6,5},{7,4},{8,11},{9,10},{10,... | collective-permute-start | bytes 86024 | tf_op jit(solution)/shard_map/ppermute | solution.py:348
  32.1 1.6 %collective-permute-done.9.refs_3_ = bf16[2,7,8,128]{3,2,1,0:T(8,128)(2,1)S(1)} collective-permute-done((bf16[2,7,8,128]{3,2,1,0:T(8,128)(2,1)}, bf16[2,7,8,128]{3,2,1,0:T(8,128)(2,1)S(1)}, u32[]{:S(2)}, u32[]{:S(2)}) %collective-permute-start.9) | collective-permute-done | bytes 28704 | tf_op jit(solution)/shard_map/ppermute | solution.py:348
  33.8 2.0 %collective-permute-done.8.refs_2_ = bf16[2,7,8,128]{3,2,1,0:T(8,128)(2,1)S(1)} collective-permute-done((bf16[2,7,8,128]{3,2,1,0:T(8,128)(2,1)}, bf16[2,7,8,128]{3,2,1,0:T(8,128)(2,1)S(1)}, u32[]{:S(2)}, u32[]{:S(2)}) %collective-permute-start.8) | collective-permute-done | bytes 28704 | tf_op jit(solution)/shard_map/ppermute | solution.py:348
  36.9 1.8 %shard_map.96 = (bf16[32,896]{1,0:T(8,128)(2,1)}, bf16[32,896]{1,0:T(8,128)(2,1)}, bf16[32,896]{1,0:T(8,128)(2,1)}, bf16[32,896]{1,0:T(8,128)(2,1)}) custom-call(bf16[2,7,8,128]{3,2,1,0:T(8,128)(2,1)} %shard_map.95.refs_0_, bf16[2,7,8,128]{3,2,1,0:T(8,128)(2,1)} %copy-done.12, bf16[2,7,8,128]{3,2,1,0:T(8,128)(2,1)} %copy-done.11, ...), custom_call_target="tpu_custom_call" | custom-call | bytes 344064 | tf_op jit(solution)/shard_map/pallas_call | solution.py:337
  39.5 9.8 %shard_map.97 = (bf16[6,6,32,128]{3,2,1,0:T(8,128)(2,1)}, bf16[6,6,32,128]{3,2,1,0:T(8,128)(2,1)}, f32[2,8,896]{2,1,0:T(8,128)}, f32[2,8,896]{2,1,0:T(8,128)}, f...) custom-call(bf16[2,4,4,32,128]{4,3,2,1,0:T(8,128)(2,1)} %get-tuple-element.37.core, bf16[2,4,2,32,128]{4,3,2,1,0:T(8,128)(2,1)} %copy-done.1, ...), custom_call_target="tpu_custom_call" | custom-call | flops 763363328 | bytes 1982464 | tf_op jit(solution)/shard_map/pallas_call | solution.py:337
  49.3 1.7 %collective-permute-start.14 = (f32[2,8,896]{2,1,0:T(8,128)}, f32[2,8,896]{2,1,0:T(8,128)S(1)}, u32[]{:S(2)}, u32[]{:S(2)}) collective-permute-start(f32[2,8,896]{2,1,0:T(8,128)} %get-tuple-element.56), channel_id=1, source_target_pairs={{0,2},{1,3},{2,0},{3,1},{4,6},{5,7},{6,4},{7,5},{8,10},{9,11},{10,... | collective-permute-start | bytes 172040 | tf_op jit(solution)/shard_map/ppermute | solution.py:348
  51.1 2.7 %collective-permute-start.15 = (f32[2,8,896]{2,1,0:T(8,128)}, f32[2,8,896]{2,1,0:T(8,128)S(1)}, u32[]{:S(2)}, u32[]{:S(2)}) collective-permute-start(f32[2,8,896]{2,1,0:T(8,128)} %get-tuple-element.57), channel_id=1, source_target_pairs={{0,3},{1,2},{2,1},{3,0},{4,7},{5,6},{6,5},{7,4},{8,11},{9,10},{10,... | collective-permute-start | bytes 172040 | tf_op jit(solution)/shard_map/ppermute | solution.py:348
  55.2 2.1 %collective-permute-done.15 = f32[2,8,896]{2,1,0:T(8,128)S(1)} collective-permute-done((f32[2,8,896]{2,1,0:T(8,128)}, f32[2,8,896]{2,1,0:T(8,128)S(1)}, u32[]{:S(2)}, u32[]{:S(2)}) %collective-permute-start.15) | collective-permute-done | bytes 57376 | tf_op jit(solution)/shard_map/ppermute | solution.py:348
  58.1 1.6 %collective-permute-start.16 = (f32[2,8,896]{2,1,0:T(8,128)S(1)}, f32[2,8,896]{2,1,0:T(8,128)S(1)}, u32[]{:S(2)}, u32[]{:S(2)}) collective-permute-start(f32[2,8,896]{2,1,0:T(8,128)S(1)} %add_add_fusion), channel_id=1, source_target_pairs={{0,4},{4,0},{1,5},{5,1},{2,6},{6,2},{3,7},{7,3},{8,12},{12,8},{9,1... | collective-permute-start | bytes 172040 | tf_op jit(solution)/shard_map/ppermute | solution.py:348
  59.7 2.7 %collective-permute-done.16 = f32[2,8,896]{2,1,0:T(8,128)S(1)} collective-permute-done((f32[2,8,896]{2,1,0:T(8,128)S(1)}, f32[2,8,896]{2,1,0:T(8,128)S(1)}, u32[]{:S(2)}, u32[]{:S(2)}) %collective-permute-start.16) | collective-permute-done | bytes 57376 | tf_op jit(solution)/shard_map/ppermute | solution.py:348
  62.5 4.1 %shard_map.98 = (bf16[4,2,4,8,128]{4,3,2,1,0:T(8,128)(2,1)}, bf16[4,2,4,8,128]{4,3,2,1,0:T(8,128)(2,1)}, bf16[4,2,4,8,128]{4,3,2,1,0:T(8,128)(2,1)}, bf16[4,2,4,8,128]{4,3,2,1,0:T(8,128)(2,1)}) custom-call(bf16[6,6,32,128]{3,2,1,0:T(8,128)(2,1)} %get-tuple-element.44.hid_ref, bf16[6,6,32,128]{3,2,1,0:T(8,128)(2,1)} %get-tuple-element.45.pre_ref, ...), custom_call_target="tpu_custom_call" | custom-call | flops 234881024 | bytes 966656 | tf_op jit(solution)/shard_map/pallas_call | solution.py:337
  66.6 3.2 %collective-permute-start.11 = (bf16[4,2,4,8,128]{4,3,2,1,0:T(8,128)(2,1)}, bf16[4,2,4,8,128]{4,3,2,1,0:T(8,128)(2,1)S(1)}, u32[]{:S(2)}, u32[]{:S(2)}) collective-permute-start(bf16[4,2,4,8,128]{4,3,2,1,0:T(8,128)(2,1)} %get-tuple-element.50), channel_id=1, source_target_pairs={{0,2},{1,3},{2,0},{3,1},{4,6},{5,7},{6,4},{7,5},{8,10},{9,11},{10,... | collective-permute-start | bytes 196616 | tf_op jit(solution)/shard_map/ppermute | solution.py:348
  72.4 1.8 %collective-permute-done.11.refs_2_ = bf16[4,2,4,8,128]{4,3,2,1,0:T(8,128)(2,1)S(1)} collective-permute-done((bf16[4,2,4,8,128]{4,3,2,1,0:T(8,128)(2,1)}, bf16[4,2,4,8,128]{4,3,2,1,0:T(8,128)(2,1)S(1)}, u32[]{:S(2)}, u32[]{:S(2)}) %collective-permute-start.11) | collective-permute-done | bytes 65568 | tf_op jit(solution)/shard_map/ppermute | solution.py:348
  74.2 1.9 %collective-permute-done.12.refs_3_ = bf16[4,2,4,8,128]{4,3,2,1,0:T(8,128)(2,1)S(1)} collective-permute-done((bf16[4,2,4,8,128]{4,3,2,1,0:T(8,128)(2,1)}, bf16[4,2,4,8,128]{4,3,2,1,0:T(8,128)(2,1)S(1)}, u32[]{:S(2)}, u32[]{:S(2)}) %collective-permute-start.12) | collective-permute-done | bytes 65568 | tf_op jit(solution)/shard_map/ppermute | solution.py:348
  76.7 1.7 %shard_map.99 = (bf16[8,4,16,128]{3,2,1,0:T(8,128)(2,1)}, bf16[8,4,16,128]{3,2,1,0:T(8,128)(2,1)}) custom-call(bf16[4,2,4,8,128]{4,3,2,1,0:T(8,128)(2,1)} %get-tuple-element.48.refs_0_, bf16[4,2,4,8,128]{4,3,2,1,0:T(8,128)(2,1)} %copy-done.3, bf16[4,2,4,8,128]{4,3,2,1,0:T(8,128)(2,1)} %copy-done.4, bf16[4,2,4,8,128]{4,3,2,1,0:T(8,128)(2,1)} %copy-done.5), custom_call_target="tpu_custom_call" | custom-call | bytes 524288 | tf_op jit(solution)/shard_map/pallas_call | solution.py:337
  79.0 1.6 %shard_map.100 = (f32[27,8,32]{2,1,0:T(8,128)}, f32[27,8,32]{2,1,0:T(8,128)}, f32[8,1]{1,0:T(8,128)}) custom-call(f32[2,8,896]{2,1,0:T(8,128)} %copy-done, f32[2,8,896]{2,1,0:T(8,128)} %copy-done.9), custom_call_target="tpu_custom_call" | custom-call | bytes 170016 | tf_op jit(solution)/shard_map/pallas_call | solution.py:337
  (57 shorter events, 16.8 us)
Async XLA Ops:
  2.5 5.6 %collective-permute-start = (bf16[4,2,4,8,128]{4,3,2,1,0:T(8,128)(2,1)}, bf16[4,2,4,8,128]{4,3,2,1,0:T(8,128)(2,1)S(1)}, u32[]{:S(2)}, u32[]{:S(2)}) collective-permute-start(bf16[4,2,4,8,128]{4,3,2,1,0:T(8,128)(2,1)} %get-tuple-element.34), channel_id=1, source_target_pairs={{0,1},{1,0},{2,3},{3,2},{4,5},{5,4},{6,7},{7,6},{8,9},{9,8},{10,11... | collective-permute-start | bytes 196616 | tf_op jit(solution)/shard_map/ppermute | solution.py:348
  5.5 7.5 %collective-permute-start.1 = (bf16[4,2,4,8,128]{4,3,2,1,0:T(8,128)(2,1)}, bf16[4,2,4,8,128]{4,3,2,1,0:T(8,128)(2,1)S(1)}, u32[]{:S(2)}, u32[]{:S(2)}) collective-permute-start(bf16[4,2,4,8,128]{4,3,2,1,0:T(8,128)(2,1)} %get-tuple-element.35), channel_id=1, source_target_pairs={{0,2},{1,3},{2,0},{3,1},{4,6},{5,7},{6,4},{7,5},{8,10},{9,11},{10,... | collective-permute-start | bytes 196616 | tf_op jit(solution)/shard_map/ppermute | solution.py:348
  8.1 6.3 %collective-permute-start.2 = (bf16[4,2,4,8,128]{4,3,2,1,0:T(8,128)(2,1)}, bf16[4,2,4,8,128]{4,3,2,1,0:T(8,128)(2,1)S(1)}, u32[]{:S(2)}, u32[]{:S(2)}) collective-permute-start(bf16[4,2,4,8,128]{4,3,2,1,0:T(8,128)(2,1)} %get-tuple-element.36), channel_id=1, source_target_pairs={{0,3},{1,2},{2,1},{3,0},{4,7},{5,6},{6,5},{7,4},{8,11},{9,10},{10,... | collective-permute-start | bytes 196616 | tf_op jit(solution)/shard_map/ppermute | solution.py:348
  8.1 6.3 %copy-start.6 = (bf16[4,2,4,8,128]{4,3,2,1,0:T(8,128)(2,1)}, bf16[4,2,4,8,128]{4,3,2,1,0:T(8,128)(2,1)S(1)}, u32[]{:S(2)}) copy-start(bf16[4,2,4,8,128]{4,3,2,1,0:T(8,128)(2,1)S(1)} %collective-permute-done.refs_1_) | copy-start | bytes 196612
  16.8 5.2 %collective-permute-start.3 = (bf16[2,4,2,32,128]{4,3,2,1,0:T(8,128)(2,1)}, bf16[2,4,2,32,128]{4,3,2,1,0:T(8,128)(2,1)S(1)}, u32[]{:S(2)}, u32[]{:S(2)}) collective-permute-start(bf16[2,4,2,32,128]{4,3,2,1,0:T(8,128)(2,1)} %get-tuple-element.38), channel_id=1, source_target_pairs={{0,1},{1,0},{2,3},{3,2},{7,6},{6,7},{5,4},{4,5},{8,9},{9,8},{10,11... | collective-permute-start | bytes 393224 | tf_op jit(solution)/shard_map/ppermute | solution.py:348
  16.8 5.2 %collective-permute-start.4 = (bf16[2,4,2,32,128]{4,3,2,1,0:T(8,128)(2,1)}, bf16[2,4,2,32,128]{4,3,2,1,0:T(8,128)(2,1)S(1)}, u32[]{:S(2)}, u32[]{:S(2)}) collective-permute-start(bf16[2,4,2,32,128]{4,3,2,1,0:T(8,128)(2,1)} %get-tuple-element.39), channel_id=1, source_target_pairs={{0,4},{1,2},{2,1},{3,7},{7,3},{6,5},{5,6},{4,0},{8,12},{9,10},{10,... | collective-permute-start | bytes 393224 | tf_op jit(solution)/shard_map/ppermute | solution.py:348
  24.6 14.1 %collective-permute-start.5 = (bf16[2,2,8,32,128]{4,3,2,1,0:T(8,128)(2,1)}, bf16[2,2,8,32,128]{4,3,2,1,0:T(8,128)(2,1)S(1)}, u32[]{:S(2)}, u32[]{:S(2)}) collective-permute-start(bf16[2,2,8,32,128]{4,3,2,1,0:T(8,128)(2,1)} %get-tuple-element.40), channel_id=1, source_target_pairs={{0,8},{8,0},{16,24},{24,16},{1,9},{9,1},{17,25},{25,17},{2,10},{10... | collective-permute-start | bytes 786440 | tf_op jit(solution)/shard_map/ppermute | solution.py:348
  24.6 14.1 %collective-permute-start.6 = (bf16[2,2,8,32,128]{4,3,2,1,0:T(8,128)(2,1)}, bf16[2,2,8,32,128]{4,3,2,1,0:T(8,128)(2,1)S(1)}, u32[]{:S(2)}, u32[]{:S(2)}) collective-permute-start(bf16[2,2,8,32,128]{4,3,2,1,0:T(8,128)(2,1)} %get-tuple-element.41), channel_id=1, source_target_pairs={{0,24},{8,16},{16,8},{24,0},{1,25},{9,17},{17,9},{25,1},{2,26},{10... | collective-permute-start | bytes 786440 | tf_op jit(solution)/shard_map/ppermute | solution.py:348
  27.8 6.0 %collective-permute-start.9 = (bf16[2,7,8,128]{3,2,1,0:T(8,128)(2,1)}, bf16[2,7,8,128]{3,2,1,0:T(8,128)(2,1)S(1)}, u32[]{:S(2)}, u32[]{:S(2)}) collective-permute-start(bf16[2,7,8,128]{3,2,1,0:T(8,128)(2,1)} %shard_map.95.refs_0_), channel_id=1, source_target_pairs={{0,3},{1,2},{2,1},{3,0},{4,7},{5,6},{6,5},{7,4},{8,11},{9,10},{10,... | collective-permute-start | bytes 86024 | tf_op jit(solution)/shard_map/ppermute | solution.py:348
  30.8 5.0 %collective-permute-start.8 = (bf16[2,7,8,128]{3,2,1,0:T(8,128)(2,1)}, bf16[2,7,8,128]{3,2,1,0:T(8,128)(2,1)S(1)}, u32[]{:S(2)}, u32[]{:S(2)}) collective-permute-start(bf16[2,7,8,128]{3,2,1,0:T(8,128)(2,1)} %shard_map.95.refs_0_), channel_id=1, source_target_pairs={{0,2},{1,3},{2,0},{3,1},{4,6},{5,7},{6,4},{7,5},{8,10},{9,11},{10,... | collective-permute-start | bytes 86024 | tf_op jit(solution)/shard_map/ppermute | solution.py:348
  31.2 4.5 %collective-permute-start.7 = (bf16[2,7,8,128]{3,2,1,0:T(8,128)(2,1)}, bf16[2,7,8,128]{3,2,1,0:T(8,128)(2,1)S(1)}, u32[]{:S(2)}, u32[]{:S(2)}) collective-permute-start(bf16[2,7,8,128]{3,2,1,0:T(8,128)(2,1)} %shard_map.95.refs_0_), channel_id=1, source_target_pairs={{0,1},{1,0},{2,3},{3,2},{4,5},{5,4},{6,7},{7,6},{8,9},{9,8},{10,11... | collective-permute-start | bytes 86024 | tf_op jit(solution)/shard_map/ppermute | solution.py:348
  33.8 2.0 %copy-start.10 = (bf16[2,7,8,128]{3,2,1,0:T(8,128)(2,1)}, bf16[2,7,8,128]{3,2,1,0:T(8,128)(2,1)S(1)}, u32[]{:S(2)}) copy-start(bf16[2,7,8,128]{3,2,1,0:T(8,128)(2,1)S(1)} %collective-permute-done.9.refs_3_) | copy-start | bytes 86020
  49.3 4.4 %collective-permute-start.13 = (f32[2,8,896]{2,1,0:T(8,128)}, f32[2,8,896]{2,1,0:T(8,128)S(1)}, u32[]{:S(2)}, u32[]{:S(2)}) collective-permute-start(f32[2,8,896]{2,1,0:T(8,128)} %get-tuple-element.55), channel_id=1, source_target_pairs={{0,1},{1,0},{2,3},{3,2},{4,5},{5,4},{6,7},{7,6},{8,9},{9,8},{10,11... | collective-permute-start | bytes 172040 | tf_op jit(solution)/shard_map/ppermute | solution.py:348
  49.3 5.9 %collective-permute-start.14 = (f32[2,8,896]{2,1,0:T(8,128)}, f32[2,8,896]{2,1,0:T(8,128)S(1)}, u32[]{:S(2)}, u32[]{:S(2)}) collective-permute-start(f32[2,8,896]{2,1,0:T(8,128)} %get-tuple-element.56), channel_id=1, source_target_pairs={{0,2},{1,3},{2,0},{3,1},{4,6},{5,7},{6,4},{7,5},{8,10},{9,11},{10,... | collective-permute-start | bytes 172040 | tf_op jit(solution)/shard_map/ppermute | solution.py:348
  51.1 6.3 %collective-permute-start.15 = (f32[2,8,896]{2,1,0:T(8,128)}, f32[2,8,896]{2,1,0:T(8,128)S(1)}, u32[]{:S(2)}, u32[]{:S(2)}) collective-permute-start(f32[2,8,896]{2,1,0:T(8,128)} %get-tuple-element.57), channel_id=1, source_target_pairs={{0,3},{1,2},{2,1},{3,0},{4,7},{5,6},{6,5},{7,4},{8,11},{9,10},{10,... | collective-permute-start | bytes 172040 | tf_op jit(solution)/shard_map/ppermute | solution.py:348
  58.1 4.2 %collective-permute-start.16 = (f32[2,8,896]{2,1,0:T(8,128)S(1)}, f32[2,8,896]{2,1,0:T(8,128)S(1)}, u32[]{:S(2)}, u32[]{:S(2)}) collective-permute-start(f32[2,8,896]{2,1,0:T(8,128)S(1)} %add_add_fusion), channel_id=1, source_target_pairs={{0,4},{4,0},{1,5},{5,1},{2,6},{6,2},{3,7},{7,3},{8,12},{12,8},{9,1... | collective-permute-start | bytes 172040 | tf_op jit(solution)/shard_map/ppermute | solution.py:348
  62.4 8.6 %collective-permute-start.17 = (f32[2,8,896]{2,1,0:T(8,128)S(1)}, f32[2,8,896]{2,1,0:T(8,128)S(1)}, u32[]{:S(2)}, u32[]{:S(2)}) collective-permute-start(f32[2,8,896]{2,1,0:T(8,128)S(1)} %add.18), channel_id=1, source_target_pairs={{0,8},{8,0},{16,24},{24,16},{1,9},{9,1},{17,25},{25,17},{2,10},{10... | collective-permute-start | bytes 172040 | tf_op jit(solution)/shard_map/ppermute | solution.py:348
  66.6 5.8 %collective-permute-start.10 = (bf16[4,2,4,8,128]{4,3,2,1,0:T(8,128)(2,1)}, bf16[4,2,4,8,128]{4,3,2,1,0:T(8,128)(2,1)S(1)}, u32[]{:S(2)}, u32[]{:S(2)}) collective-permute-start(bf16[4,2,4,8,128]{4,3,2,1,0:T(8,128)(2,1)} %get-tuple-element.49), channel_id=1, source_target_pairs={{0,1},{1,0},{2,3},{3,2},{4,5},{5,4},{6,7},{7,6},{8,9},{9,8},{10,11... | collective-permute-start | bytes 196616 | tf_op jit(solution)/shard_map/ppermute | solution.py:348
  66.6 7.6 %collective-permute-start.11 = (bf16[4,2,4,8,128]{4,3,2,1,0:T(8,128)(2,1)}, bf16[4,2,4,8,128]{4,3,2,1,0:T(8,128)(2,1)S(1)}, u32[]{:S(2)}, u32[]{:S(2)}) collective-permute-start(bf16[4,2,4,8,128]{4,3,2,1,0:T(8,128)(2,1)} %get-tuple-element.50), channel_id=1, source_target_pairs={{0,2},{1,3},{2,0},{3,1},{4,6},{5,7},{6,4},{7,5},{8,10},{9,11},{10,... | collective-permute-start | bytes 196616 | tf_op jit(solution)/shard_map/ppermute | solution.py:348
  69.8 6.3 %collective-permute-start.12 = (bf16[4,2,4,8,128]{4,3,2,1,0:T(8,128)(2,1)}, bf16[4,2,4,8,128]{4,3,2,1,0:T(8,128)(2,1)S(1)}, u32[]{:S(2)}, u32[]{:S(2)}) collective-permute-start(bf16[4,2,4,8,128]{4,3,2,1,0:T(8,128)(2,1)} %get-tuple-element.51), channel_id=1, source_target_pairs={{0,3},{1,2},{2,1},{3,0},{4,7},{5,6},{6,5},{7,4},{8,11},{9,10},{10,... | collective-permute-start | bytes 196616 | tf_op jit(solution)/shard_map/ppermute | solution.py:348
  71.0 7.4 %copy-start = (f32[2,8,896]{2,1,0:T(8,128)}, f32[2,8,896]{2,1,0:T(8,128)S(1)}, u32[]{:S(2)}) copy-start(f32[2,8,896]{2,1,0:T(8,128)S(1)} %add.19.own_ref) | copy-start | bytes 172036
  71.0 7.4 %collective-permute-start.18 = (f32[2,8,896]{2,1,0:T(8,128)S(1)}, f32[2,8,896]{2,1,0:T(8,128)S(1)}, u32[]{:S(2)}, u32[]{:S(2)}) collective-permute-start(f32[2,8,896]{2,1,0:T(8,128)S(1)} %add.19.own_ref), channel_id=1, source_target_pairs={{0,16},{8,24},{16,0},{24,8},{1,17},{9,25},{17,1},{25,9},{2,18},{10... | collective-permute-start | bytes 172040 | tf_op jit(solution)/shard_map/ppermute | solution.py:348
  72.4 3.7 %copy-start.3 = (bf16[4,2,4,8,128]{4,3,2,1,0:T(8,128)(2,1)}, bf16[4,2,4,8,128]{4,3,2,1,0:T(8,128)(2,1)S(1)}, u32[]{:S(2)}) copy-start(bf16[4,2,4,8,128]{4,3,2,1,0:T(8,128)(2,1)S(1)} %collective-permute-done.10.refs_1_) | copy-start | bytes 196612
  74.2 1.9 %copy-start.4 = (bf16[4,2,4,8,128]{4,3,2,1,0:T(8,128)(2,1)}, bf16[4,2,4,8,128]{4,3,2,1,0:T(8,128)(2,1)S(1)}, u32[]{:S(2)}) copy-start(bf16[4,2,4,8,128]{4,3,2,1,0:T(8,128)(2,1)S(1)} %collective-permute-done.11.refs_2_) | copy-start | bytes 196612
  (10 other events, 7.3 us)
where the time goes:
time: 82.5 us; the launch traced here: 82 us
  Pallas kernels  26.1 us (32%)
  waiting for transfers between devices  24.3 us (29%)
  starting transfers between devices  24.1 us (29%)
  local copies, waits for them, and re-layouts  4.53 us (5%)
  other arithmetic  2.16 us (3%)
    pallas_call x9, Pallas kernels, call(): pl.pallas_call(body, out_shape=tuple(outs), in_specs=specs or [pl.BlockSp...  26.1 us
    ppermute x19, waiting for transfers between devices, swap(): return lax.ppermute(value, axes, pairs)  24.3 us
    ppermute x19, starting transfers between devices, swap(): return lax.ppermute(value, axes, pairs)  24.1 us
    unnamed x30, local copies, waits for them, and re-layouts  4.53 us
  transfers between devices with their start and end apart: 19, of which 11 were waited for; matrix products, arithmetic and copies ran while one was open for 0% of the time, Pallas kernels for 11%

commit v1 on v0

v1 whole, which is shorter than its diff:
```python
import functools
import math

import jax
import jax.numpy as jnp
from jax import lax
from jax.experimental import pallas as pl
from jax.experimental.pallas import tpu as pltpu
from jax.sharding import PartitionSpec as P


BF = jnp.bfloat16
F32 = jnp.float32
LIMIT = 20 << 20
RIM = 2


def place(sizes):
    me = lax.axis_index("af")
    row = lax.axis_index("gy")
    part = part_of(me, row, sizes)
    return me, row, part, row * sizes["af"] + part


def part_of(chan, row, sizes):
    return jnp.where(row % 2 == 0, chan, sizes["af"] - 1 - chan)


def own_order(parts, me):
    bit = 1
    while bit < len(parts):
        turn = (me & bit) != 0
        parts = [lax.select(turn, parts[g ^ bit], parts[g]) for g in range(len(parts))]
        bit *= 2
    return parts


def pack_body(sizes, vol_hbm, cot_hbm, one_hbm, two_hbm, bias_hbm, *refs):
    groups = sizes["af"]
    outs = refs[:groups]
    vol_ref, cot_ref, one_ref, two_ref, bias_ref, flat, turned, packed, sems = refs[groups:]
    chans, nx, ny, nz = vol_ref.shape
    rows = ny // groups
    me, row, _, _ = place(sizes)
    pairs = (
        (one_hbm, one_ref),
        (two_hbm, two_ref),
        (bias_hbm, bias_ref),
        (vol_hbm, vol_ref),
        (cot_hbm, cot_ref),
    )
    copies = [pltpu.make_async_copy(src, dst, sems.at[n]) for n, (src, dst) in enumerate(pairs)]
    for copy in copies:
        copy.start()
    for copy in copies[:3]:
        copy.wait()
    pack_weights(one_ref, two_ref, bias_ref, packed)
    core = lax.axis_index("gx") % 2
    cells = rows * 2 * nx
    for a, ref in enumerate((vol_ref, cot_ref)):
        copies[3 + a].wait()
        for x in range(nx):
            flat[a, x] = ref[:, x].astype(F32).reshape(chans * ny, nz)
        for x in range(nx):
            for y in range(ny):
                turned[y, a, x] = flat[a, x, pl.ds(y, chans, stride=ny), :].astype(BF)
    for s in range(groups):
        start = part_of(me ^ s, row, sizes) * rows
        for r in range(rows):
            for a in range(2):
                for x in range(nx):
                    outs[s][(r * 2 + a) * nx + x] = turned[start + r, a, x]
        outs[s][cells:] = packed[core]


def rim_starts(even, size):
    first = jnp.where(even, RIM + size, 0)
    return first, RIM + size - first


def rim_source(even, size):
    first = jnp.where(even, size - RIM, 0)
    return first, size - RIM - first


def clear_wrap(ref, spot, spots):
    @pl.when(jnp.logical_or(spot == 0, spot == spots - 1))
    def _():
        ref[...] = jnp.zeros_like(ref)


def join_body(sizes, parts_shape, *refs):
    groups = sizes["af"]
    rows, fields, nx = parts_shape
    parts, (core_ref, y_one, y_two, x_one, x_two, weight_ref) = refs[:groups], refs[groups:]
    me, _, _, spot = place(sizes)
    gx = lax.axis_index("gx")

    def whole(n):
        cells = own_order([p[n].astype(F32) for p in parts], me)
        return jnp.concatenate(cells, axis=0).astype(BF)

    for a in range(fields):
        for x in range(nx):
            for y in range(rows):
                core_ref[a, x, y] = whole((y * fields + a) * nx + x)
    for ref, start in zip((y_one, y_two), rim_source(spot % 2 == 0, rows)):
        for a in range(fields):
            for x in range(nx):
                for h in range(RIM):
                    ref[a, x, h] = core_ref[a, x, start + h]
    for ref, start in zip((x_one, x_two), rim_source(gx % 2 == 0, nx)):
        for a in range(fields):
            for h in range(RIM):
                for y in range(rows):
                    ref[a, h, y] = core_ref[a, start + h, y]
    clear_wrap(y_two, spot, sizes["gy"] * groups)
    clear_wrap(x_two, gx, sizes["gx"])
    for t in range(weight_ref.shape[1] // 128):
        weight_ref[:, t * 128 : (t + 1) * 128] = whole(rows * fields * nx + t)


def edge_body(sizes, ya, yb, first_ref, second_ref):
    fields, nx = ya.shape[:2]
    spot = place(sizes)[3]
    gx = lax.axis_index("gx")
    y_first, y_second = rim_starts(spot % 2 == 0, 0)
    for ref, start in zip((first_ref, second_ref), rim_source(gx % 2 == 0, nx)):
        for a in range(fields):
            for h in range(RIM):
                for r in range(RIM):
                    ref[a, h, y_first + r] = ya[a, start + h, r]
                    ref[a, h, y_second + r] = yb[a, start + h, r]
    clear_wrap(second_ref, gx, sizes["gx"])


def pack_weights(one_ref, two_ref, bias_ref, out_ref):
    taps, chans, width = one_ref.shape
    per = 128 // width
    tiles = out_ref.shape[1]
    sub = lax.broadcasted_iota(jnp.int32, (chans, width), 0)
    lane = lax.broadcasted_iota(jnp.int32, (chans, width), 1)
    spread_bias = jnp.broadcast_to(bias_ref[...], (chans, chans))
    diagonal = sub[:, :chans] == lane[:, :chans]
    bias = jnp.sum(jnp.where(diagonal, spread_bias, 0.0), axis=1, keepdims=True)
    bias = jnp.broadcast_to(bias, (chans, width))
    top = bias.astype(BF).astype(F32)
    mid = (bias - top).astype(BF).astype(F32)
    low = bias - top - mid
    extra = jnp.where(lane == 0, top, jnp.where(lane == 1, mid, jnp.where(lane == 2, low, 0.0)))
    none = jnp.zeros_like(extra)
    for k, ref in enumerate((one_ref, two_ref)):
        for t in range(tiles):
            cells = []
            for j in range(per):
                tap = t * per + j
                if tap < taps:
                    cells.append(ref[tap].astype(F32))
                else:
                    cells.append(extra if k == 0 and tap == taps else none)
            out_ref[k, t] = jnp.concatenate(cells, axis=1).astype(BF)


def weight_join_body(taps, mine_ref, other_ref, *outs):
    width = mine_ref.shape[0]
    tiles = mine_ref.shape[1] // 128
    per = 128 // width
    first_core = lax.axis_index("gx") % 2 == 0
    for k in range(2):
        plain, turned = outs[2 * k], outs[2 * k + 1]
        blocks = {}
        for t in range(tiles):
            at = slice(t * 128, (t + 1) * 128)
            mine, other = mine_ref[:, at].astype(F32), other_ref[:, at].astype(F32)
            tile = lax.select(first_core, (mine, other)[k], (other, mine)[k])
            plain[:, at] = tile.astype(BF)
            back = tile.T
            for j in range(per):
                blocks[t * per + j] = back[j * width : (j + 1) * width]
        none = jnp.zeros((width, width), F32)
        for t in range(tiles):
            cells = []
            for j in range(per):
                tap = t * per + j
                cells.append(blocks[taps - 1 - tap] if tap < taps else none)
            turned[:, t * 128 : (t + 1) * 128] = jnp.concatenate(cells, axis=1).astype(BF)


def spread(ref, x, y, tile):
    width, nz = tile.shape
    lane = lax.broadcasted_iota(jnp.int32, tile.shape, 1)
    none = jnp.zeros_like(tile)
    ref[x, y, :width] = jnp.where(lane == 0, none, pltpu.roll(tile, 1, 1))
    ref[x, y, width : 2 * width] = tile
    ref[x, y, 2 * width :] = jnp.where(lane == nz - 1, none, pltpu.roll(tile, nz - 1, 1))


def extra_rows(width, count):
    sub = lax.broadcasted_iota(jnp.int32, (width, count), 0)
    return jnp.where(sub < 3, 1.0, 0.0).astype(BF)


def window(get, x, ys, extra):
    columns = []
    for y in ys:
        pieces = [get(x + i, y + j) for i in range(3) for j in range(3)]
        columns.append(jnp.concatenate(pieces + [extra], axis=0))
    return jnp.concatenate(columns, axis=1) if len(columns) > 1 else columns[0]


def outside(x, size, low):
    return x < low or x >= low + size


def stacked(early, late, sizes_xy, low):
    def get(x, y, rows=slice(None)):
        nx, ny = sizes_xy
        if outside(x, nx, low) and outside(y, ny, low):
            return late[x if x < low else x - nx, y if y < low else y - ny, rows]
        return early[x, y, rows]

    return get


def dot(left, right):
    return lax.dot_general(left, right, (((1,), (0,)), ((), ())), preferred_element_type=F32)


def dot_cells(left, right):
    return lax.dot_general(left, right, (((1,), (1,)), ((), ())), preferred_element_type=F32)


def layer(sizes, shape, get_vol, get_cot, one_ref, two_ref, put_hid, put_pre, x, ys, extra):
    nx, rows, nz = shape
    spot = place(sizes)[3]
    gx = lax.axis_index("gx")
    pre_acts = dot(one_ref[...], window(get_vol, x, ys, extra))
    hid_grads = dot(two_ref[...], window(get_cot, x, ys, extra))
    for n, y in enumerate(ys):
        at = slice(n * nz, (n + 1) * nz)
        pre_act = pre_acts[:, at]
        sigma = 1.0 / (1.0 + jnp.exp(-pre_act))
        slope = sigma * (1.0 + pre_act * (1.0 - sigma))
        rules = []
        if x == 0:
            rules.append(gx > 0)
        if x == nx + 1:
            rules.append(gx < sizes["gx"] - 1)
        if y == 0:
            rules.append(spot > 0)
        if y == rows + 1:
            rules.append(spot < sizes["gy"] * sizes["af"] - 1)
        for tile, put in ((pre_act * sigma, put_hid), (hid_grads[:, at] * slope, put_pre)):
            if rules:
                ok = functools.reduce(jnp.logical_and, rules)
                tile = lax.select(ok, tile, jnp.zeros_like(tile))
            put(x, y, tile.astype(BF))


def act_body(sizes, core, ya, yb, xa, xb, one_ref, two_ref, vol_s, cot_s, hid_s, pre_s):
    _, nx, rows, width, nz = core.shape
    gx = lax.axis_index("gx")
    y_first, y_second = rim_starts(place(sizes)[3] % 2 == 0, rows)
    x_first, x_second = rim_starts(gx % 2 == 0, nx)
    extra = extra_rows(width, nz)
    for a, stack in enumerate((vol_s, cot_s)):
        for x in range(nx):
            for h in range(RIM):
                spread(stack, RIM + x, y_first + h, ya[a, x, h])
                spread(stack, RIM + x, y_second + h, yb[a, x, h])
            for y in range(rows):
                spread(stack, RIM + x, RIM + y, core[a, x, y])
        for h in range(RIM):
            for y in range(rows):
                spread(stack, x_first + h, RIM + y, xa[a, h, y])
                spread(stack, x_second + h, RIM + y, xb[a, h, y])

    def get(stack):
        return lambda x, y: stack[x, y]

    def put(stack):
        return lambda x, y, tile: spread(stack, x, y, tile)

    for x in range(nx + 2):
        for start in range(0, rows + 2, 2):
            if outside(x, nx - 2, RIM) and outside(start, rows - 2, RIM):
                continue
            layer(
                sizes, (nx, rows, nz), get(vol_s), get(cot_s), one_ref, two_ref,
                put(hid_s), put(pre_s), x, [start, start + 1], extra,
            )


def fields_body(sizes, ca, cb, one_ref, two_ref, vol_e, cot_e, hid_e, pre_e, *refs):
    hid_l, pre_l, keep_ref, send_ref, vol_l, cot_l = refs
    nx, rows = (n - 2 * RIM for n in vol_e.shape[:2])
    width, nz = ca.shape[3:]
    spot = place(sizes)[3]
    gx = lax.axis_index("gx")
    extra = extra_rows(width, nz)
    x_first, x_second = rim_starts(gx % 2 == 0, 0)
    for a, stack in enumerate((vol_l, cot_l)):
        for h in range(RIM):
            for y in range(2 * RIM):
                spread(stack, x_first + h, y, ca[a, h, y])
                spread(stack, x_second + h, y, cb[a, h, y])

    get_vol = stacked(vol_e, vol_l, (nx, rows), RIM)
    get_cot = stacked(cot_e, cot_l, (nx, rows), RIM)
    get_hid = stacked(hid_e, hid_l, (nx - 2, rows - 2), RIM)
    get_pre = stacked(pre_e, pre_l, (nx - 2, rows - 2), RIM)

    def put(stack):
        def store(x, y, tile):
            spread(stack, x if x < RIM else x - nx + 2, y if y < RIM else y - rows + 2, tile)

        return store

    for x in range(nx + 2):
        for start in range(0, rows + 2, 2):
            if outside(x, nx - 2, RIM) and outside(start, rows - 2, RIM):
                layer(
                    sizes, (nx, rows, nz), get_vol, get_cot, one_ref, two_ref,
                    put(hid_l), put(pre_l), x, [start, start + 1], extra,
                )

    middle = slice(width, 2 * width)
    acc = [None, None]
    for x in range(nx):
        ys = list(range(rows))
        cot = [get_cot(RIM + x, RIM + y, middle) for y in ys]
        pre = [get_pre(1 + x, 1 + y, middle) for y in ys]
        got = (
            dot_cells(jnp.concatenate(cot, axis=1), window(get_hid, x, ys, extra)),
            dot_cells(
                jnp.concatenate(pre, axis=1),
                window(get_vol, x + 1, [y + 1 for y in ys], extra),
            ),
        )
        acc = [g if old is None else old + g for old, g in zip(acc, got)]

    first_core = gx % 2 == 0
    keep_ref[...] = lax.select(first_core, acc[0], acc[1])
    send_ref[...] = lax.select(first_core, acc[1], acc[0])


def split_body(sizes, own_ref, got_ref, keep_ref, send_ref, total):
    groups = sizes["af"]
    me = lax.axis_index("af")
    chans = own_ref.shape[0] // groups
    for g in range(groups):
        rows = slice(g * chans, (g + 1) * chans)
        total[g] = own_ref[rows] + got_ref[rows]
    for j in range(groups // 2):
        keep_ref[j] = total[me ^ (2 * j)]
        send_ref[j] = total[me ^ (2 * j + 1)]


def halve_body(own_ref, got_ref, keep_ref, send_ref):
    for j in range(own_ref.shape[0] // 2):
        keep_ref[j] = own_ref[2 * j] + got_ref[2 * j]
        send_ref[j] = own_ref[2 * j + 1] + got_ref[2 * j + 1]


def sum_body(*refs):
    parts = [ref[...] for ref in refs[:-1]]
    while len(parts) > 1:
        parts = [parts[i] + parts[i + 1] for i in range(0, len(parts), 2)]
    refs[-1][...] = parts[0]


def outputs_body(sizes, hid_e, pre_e, hid_l, pre_l, two_ref, one_ref, *refs):
    groups = sizes["af"]
    outs, (turned,) = refs[:groups], refs[groups:]
    nx, rows = (n - 2 for n in hid_e.shape[:2])
    width, nz = two_ref.shape[0], hid_e.shape[3]
    chans = width // groups
    me = lax.axis_index("af")
    extra = jnp.zeros((width, nz), BF)
    get_hid = stacked(hid_e, hid_l, (nx - 2, rows - 2), RIM)
    get_pre = stacked(pre_e, pre_l, (nx - 2, rows - 2), RIM)
    for x in range(nx):
        for start in range(0, rows, 2):
            ys = [start, start + 1]
            for a, (ref, get) in enumerate(((two_ref, get_hid), (one_ref, get_pre))):
                got = dot(ref[...], window(get, x, ys, extra))
                for n, y in enumerate(ys):
                    for g in range(groups):
                        turned[g, y, a, x] = got[
                            g * chans : (g + 1) * chans, n * nz : (n + 1) * nz
                        ].astype(BF)
    for s in range(groups):
        outs[s][...] = turned[me ^ s]


def unpack_body(sizes, *refs):
    groups = sizes["af"]
    parts, (out_ref, grad_ref, flat) = refs[:groups], refs[groups:]
    rows, _, nx, chans, _ = parts[0].shape
    ny = rows * groups
    me, row, _, _ = place(sizes)
    for s in range(groups):
        start = part_of(me ^ s, row, sizes) * rows
        for y in range(rows):
            for a in range(2):
                for x in range(nx):
                    spot = pl.multiple_of((start + y) * chans, chans)
                    flat[a, x, pl.ds(spot, chans), :] = parts[s][y, a, x].astype(F32)
    for a, ref in enumerate((out_ref, grad_ref)):
        for x in range(nx):
            for c in range(chans):
                ref[c, x] = flat[a, x, pl.ds(c, ny, stride=chans), :].astype(BF)


def total_body(scale, taps, width, own_ref, got_ref, one_ref, two_ref, bias_ref):
    first_core = lax.axis_index("gx") % 2 == 0
    own, got = own_ref[0] * scale, got_ref[0] * scale
    chans = own.shape[0]
    two, one = lax.select(first_core, own, got), lax.select(first_core, got, own)
    for total, ref in ((one, one_ref), (two, two_ref)):
        for tap in range(taps):
            ref[tap] = total[:, tap * width : (tap + 1) * width]
    bias = jnp.broadcast_to(one[:, taps * width : taps * width + 1], (chans, chans))
    sub = lax.broadcasted_iota(jnp.int32, (chans, chans), 0)
    lane = lax.broadcasted_iota(jnp.int32, (chans, chans), 1)
    bias_ref[...] = jnp.sum(jnp.where(sub == lane, bias, 0.0), axis=0, keepdims=True)


def call(body, outs, scratch, args, specs=None, flops=0):
    moved = sum(math.prod(a.shape) * a.dtype.itemsize for a in args)
    moved += sum(math.prod(o.shape) * o.dtype.itemsize for o in outs)
    return pl.pallas_call(
        body,
        out_shape=tuple(outs),
        in_specs=specs or [pl.BlockSpec(memory_space=pltpu.VMEM)] * len(args),
        out_specs=tuple(pl.BlockSpec(memory_space=pltpu.VMEM) for _ in outs),
        scratch_shapes=scratch,
        compiler_params=pltpu.CompilerParams(vmem_limit_bytes=LIMIT),
        cost_estimate=pl.CostEstimate(flops=flops, bytes_accessed=moved, transcendentals=0),
    )(*args)


def across(value, step, sizes):
    return lax.ppermute(value, "af", [(i, i ^ step) for i in range(sizes["af"])])


def ring_pairs(count, second):
    if not second:
        return [(i, i ^ 1) for i in range(count)]
    return [(i, ((((i - 1) % count) ^ 1) + 1) % count) for i in range(count)]


def y_pairs(sizes, second):
    groups = sizes["af"]

    def spot(i):
        row, part = divmod(i, groups)
        return row * groups + (part if row % 2 == 0 else groups - 1 - part)

    pairs = ring_pairs(sizes["gy"] * groups, second)
    return [(spot(i), spot(j)) for i, j in pairs]


def body(sizes, volume, weight_one, bias_one, weight_two, cotangent):
    groups = sizes["af"]
    chans, nx, ny, nz = volume.shape
    width = chans * groups
    rows = ny // groups
    taps = 27
    tiles = -(-(taps + 1) * width // 128)
    columns = tiles * 128
    bind = functools.partial
    shape = jax.ShapeDtypeStruct
    far = range(groups - 1, 0, -1)

    cores = ring_pairs(sizes["gx"], False)

    def exchange(pieces):
        got = {s: across(pieces[s], s, sizes) for s in far}
        return [pieces[0]] + [got[s] for s in range(1, groups)]

    piece = shape((rows, 2, nx, chans, nz), BF)
    in_taps = [
        jnp.transpose(w, (2, 3, 4, 0, 1)).reshape(taps, chans, width)
        for w in (weight_one, weight_two)
    ]
    args = (volume, cotangent, *in_taps, bias_one.reshape(1, chans))
    parcel = shape((rows * 2 * nx + tiles, chans, 128), BF)
    sent = call(
        bind(pack_body, sizes),
        [parcel] * groups,
        [
            pltpu.VMEM((chans, nx, ny, nz), BF),
            pltpu.VMEM((chans, nx, ny, nz), BF),
            pltpu.VMEM((taps, chans, width), BF),
            pltpu.VMEM((taps, chans, width), BF),
            pltpu.VMEM((1, chans), F32),
            pltpu.VMEM((2, nx, chans * ny, nz), F32),
            pltpu.VMEM((ny, 2, nx, chans, nz), BF),
            pltpu.VMEM((2, tiles, chans, 128), BF),
            pltpu.SemaphoreType.DMA((5,)),
        ],
        tuple(pltpu.with_memory_space_constraint(v, pltpu.HBM) for v in args),
        [pl.BlockSpec(memory_space=pltpu.HBM)] * 5,
    )
    parts = exchange(sent)

    y_rim = shape((2, nx, RIM, width, nz), BF)
    x_rim = shape((2, RIM, rows, width, nz), BF)
    flat_w = shape((width, columns), BF)
    core, y_one, y_two, x_one, x_two, mine = call(
        bind(join_body, sizes, (rows, 2, nx)),
        [shape((2, nx, rows, width, nz), BF), y_rim, y_rim, x_rim, x_rim, flat_w],
        [],
        parts,
    )
    near, wrap = ring_pairs(sizes["gx"], False), ring_pairs(sizes["gx"], True)
    y_rims = (
        lax.ppermute(y_one, ("gy", "af"), y_pairs(sizes, False)),
        lax.ppermute(y_two, ("gy", "af"), y_pairs(sizes, True)),
    )
    x_rims = lax.ppermute(x_one, "gx", near), lax.ppermute(x_two, "gx", wrap)
    other = lax.ppermute(mine, "gx", cores)

    corner = shape((2, RIM, 2 * RIM, width, nz), BF)
    c_one, c_two = call(bind(edge_body, sizes), [corner] * 2, [], y_rims)
    corners = lax.ppermute(c_one, "gx", near), lax.ppermute(c_two, "gx", wrap)
    one, one_t, two, two_t = call(
        bind(weight_join_body, taps), [flat_w] * 4, [], (mine, other)
    )

    stack = shape((nx + 2 * RIM, rows + 2 * RIM, 3 * width, nz), BF)
    field = shape((nx + 2, rows + 2, 3 * width, nz), BF)
    late = shape((2 * RIM, 2 * RIM, 3 * width, nz), BF)
    share = shape((width, columns), F32)
    stacks = call(
        bind(act_body, sizes),
        [stack, stack, field, field],
        [],
        (core, *y_rims, *x_rims, one, two_t),
        flops=2 * width * columns * nz * (nx + 2) * (rows + 2),
    )
    hid_l, pre_l, keep, send = call(
        bind(fields_body, sizes),
        [late, late, share, share],
        [pltpu.VMEM(late.shape, BF), pltpu.VMEM(late.shape, BF)],
        (*corners, one, two_t, *stacks),
        flops=2 * width * columns * nz * ((nx + 2) * (rows + 2) + 2 * nx * rows),
    )

    half = shape((groups // 2, chans, columns), F32)
    got = lax.ppermute(send, "gx", cores)
    keep, send = call(
        bind(split_body, sizes),
        [half, half],
        [pltpu.VMEM((groups, chans, columns), F32)],
        (keep, got),
    )
    bit = 1
    while bit < groups:
        got = across(send, bit, sizes)
        if 2 * bit < groups:
            half = shape((groups // (4 * bit), chans, columns), F32)
            keep, send = call(halve_body, [half, half], [], (keep, got))
        bit *= 2

    pieces = call(
        bind(outputs_body, sizes),
        [piece] * groups,
        [pltpu.VMEM((groups, rows, 2, nx, chans, nz), BF)],
        (*stacks[2:], hid_l, pre_l, two, one_t),
        flops=4 * width * columns * nz * nx * rows,
    )

    own = shape((1, chans, columns), F32)
    (total,) = call(sum_body, [own], [], (keep, got))
    bits = []
    for axis, low in (("gx", 2), ("gy", 1)):
        while low < sizes[axis]:
            bits.append((low if axis == "gy" else low * sizes["gy"]))
            low *= 2
    while bits:
        steps = [0]
        for bit in bits[:2]:
            steps += [step ^ bit for step in steps]
        bits = bits[2:]
        count = sizes["gx"] * sizes["gy"]
        got = [
            lax.ppermute(total, ("gx", "gy"), [(i, i ^ step) for i in range(count)])
            for step in steps[1:]
        ]
        (total,) = call(sum_body, [own], [], [total, *got])
    last = lax.ppermute(total, "gx", cores)

    pieces = exchange(pieces)
    block = shape((chans, nx, ny, nz), BF)
    output, input_grad = call(
        bind(unpack_body, sizes),
        [block, block],
        [pltpu.VMEM((2, nx, chans * ny, nz), F32)],
        pieces,
    )

    cells = nx * sizes["gx"] * ny * sizes["gy"] * nz
    tap_grad = shape((taps, chans, width), F32)
    grad_one, grad_two, bias_grad = call(
        bind(total_body, 1.0 / math.sqrt(cells), taps, width),
        [tap_grad, tap_grad, shape((1, chans), F32)],
        [],
        (total, last),
    )

    def unturn(grad):
        return jnp.transpose(grad.reshape(3, 3, 3, chans, width), (3, 4, 0, 1, 2))

    return output, input_grad, unturn(grad_one), bias_grad.reshape(chans), unturn(grad_two)


def solution(mesh):
    def run(*args):
        return body(dict(mesh.shape), *args)

    return jax.shard_map(
        run,
        mesh=mesh,
        in_specs=(
            P("af", "gx", "gy", None),
            P("af", None, None, None, None),
            P("af"),
            P("af", None, None, None, None),
            P("af", "gx", "gy", None),
        ),
        out_specs=(
            P("af", "gx", "gy", None),
            P("af", "gx", "gy", None),
            P("af", None, None, None, None),
            P("af"),
            P("af", None, None, None, None),
        ),
        check_vma=False,
    )
```

time: 82.5 us -> 55.2 us (0.67)
  Pallas kernels: 26.1 us -> 10.1 us
  local copies, waits for them, and re-layouts: 4.53 us -> 0 us
  waiting for transfers between devices: 24.3 us -> 21.4 us
  other arithmetic: 2.16 us -> 0 us
  starting transfers between devices: 24.1 us -> 22.9 us
    pallas_call x9 -> x13, Pallas kernels: 26.1 us -> 10.1 us  [call(): pl.pallas_call(body, out_shape=tuple(outs), in_specs=specs or [pl.BlockSp...]
    unnamed x30 -> x0, local copies, waits for them, and re-layouts: 4.53 us -> none
    ppermute x19 -> x20, waiting for transfers between devices: 24.3 us -> 21.4 us  [the longest x8 13.7 us: across(): lax.ppermute(value, 'af', [(i, i ^ step) for i in range(sizes['af'])])]
    pallas_call x1 -> x0, other arithmetic: 1.31 us -> none  [call(): pl.pallas_call(body, out_shape=tuple(outs), in_specs=specs or [pl.BlockSp...]
    ppermute x19 -> x20, starting transfers between devices: 24.1 us -> 22.9 us  [the longest x8 12.5 us: across(): lax.ppermute(value, 'af', [(i, i ^ step) for i in range(sizes['af'])])]
    add x3 -> x0, other arithmetic: 0.85 us -> none  [the longest x1 0.84 us: body(): total = total + across(shares[s], s, sizes)]
  transfers between devices with their start and end apart: 19 -> 20, of which waited for: 11 -> 12; matrix products, arithmetic and copies ran while one was open for 0% -> 0% of each run, Pallas kernels for 11% -> 8%
where the time goes in v1:
time: 55.2 us; the launch traced here: 55.1 us
  starting transfers between devices  22.9 us (41%)
  waiting for transfers between devices  21.4 us (39%)
  Pallas kernels  10.1 us (18%)
  between operations  0.75 us (1%)
    ppermute x8, waiting for transfers between devices, across(): lax.ppermute(value, 'af', [(i, i ^ step) for i in range(sizes['af'])])  13.7 us
    ppermute x8, starting transfers between devices, across(): lax.ppermute(value, 'af', [(i, i ^ step) for i in range(sizes['af'])])  12.5 us
    pallas_call x13, Pallas kernels, call(): pl.pallas_call(body, out_shape=tuple(outs), in_specs=specs or [pl.BlockSp...  10.1 us
    ppermute x3, starting transfers between devices, body(): lax.ppermute(total, ('gx', 'gy'), [(i, i ^ step) for i in range(count)])  3.49 us
    ppermute x3, waiting for transfers between devices, body(): lax.ppermute(total, ('gx', 'gy'), [(i, i ^ step) for i in range(count)])  3.33 us
    ppermute x2, starting transfers between devices, body(): corners = (lax.ppermute(c_one, 'gx', near), lax.ppermute(c_two, 'gx', wrap))  1.66 us
    ppermute x2, starting transfers between devices, body(): x_rims = (lax.ppermute(x_one, 'gx', near), lax.ppermute(x_two, 'gx', wrap))  1.62 us
    ppermute x1, starting transfers between devices, body(): lax.ppermute(y_two, ('gy', 'af'), y_pairs(sizes, True))  1.49 us
  transfers between devices with their start and end apart: 20, of which 12 were waited for; matrix products, arithmetic and copies ran while one was open for 0% of the time, Pallas kernels for 8%

profile of v1, /device:TPU:0, one launch (start us, length us, event | category | flops | bytes accessed | tf_op | source)
XLA Modules:
  0.0 55.1 jit_solution(18253993428871733227)
XLA Ops:
  0.6 1.3 %shard_map.92 = (bf16[39,8,128]{2,1,0:T(8,128)(2,1)S(1)}, bf16[39,8,128]{2,1,0:T(8,128)(2,1)S(1)}, bf16[39,8,128]{2,1,0:T(8,128)(2,1)S(1)}, bf16[39,8,128]{2,1,0:T(8,128)(2,1)S(1)}) custom-call(bf16[8,4,16,128]{3,2,1,0:T(8,128)(2,1)} %vol_hbm.1, bf16[8,4,16,128]{3,2,1,0:T(8,128)(2,1)} %cot_hbm.1, bf16[27,8,32]{2,1,0:T(8,128)(2,1)} %bitcast.14, ...), custom_call_target="tpu_custom_call" | custom-call | bytes 609312 | tf_op jit(solution)/shard_map/pallas_call | solution.py:432
  1.9 3.1 %collective-permute-start = (bf16[39,8,128]{2,1,0:T(8,128)(2,1)S(1)}, bf16[39,8,128]{2,1,0:T(8,128)(2,1)S(1)}, u32[]{:S(2)}, u32[]{:S(2)}) collective-permute-start(bf16[39,8,128]{2,1,0:T(8,128)(2,1)S(1)} %get-tuple-element.43), channel_id=1, source_target_pairs={{0,1},{1,0},{2,3},{3,2},{4,5},{5,4},{6,7},{7,6},{8,9},{9,8},{10,11... | collective-permute-start | bytes 239624 | tf_op jit(solution)/shard_map/ppermute | solution.py:444
  5.0 2.6 %collective-permute-start.1 = (bf16[39,8,128]{2,1,0:T(8,128)(2,1)S(1)}, bf16[39,8,128]{2,1,0:T(8,128)(2,1)S(1)}, u32[]{:S(2)}, u32[]{:S(2)}) collective-permute-start(bf16[39,8,128]{2,1,0:T(8,128)(2,1)S(1)} %get-tuple-element.44), channel_id=1, source_target_pairs={{0,2},{1,3},{2,0},{3,1},{4,6},{5,7},{6,4},{7,5},{8,10},{9,11},{10,... | collective-permute-start | bytes 239624 | tf_op jit(solution)/shard_map/ppermute | solution.py:444
  7.6 6.4 %collective-permute-done.1.refs_2_ = bf16[39,8,128]{2,1,0:T(8,128)(2,1)S(1)} collective-permute-done((bf16[39,8,128]{2,1,0:T(8,128)(2,1)S(1)}, bf16[39,8,128]{2,1,0:T(8,128)(2,1)S(1)}, u32[]{:S(2)}, u32[]{:S(2)}) %collective-permute-start.1) | collective-permute-done | bytes 79904 | tf_op jit(solution)/shard_map/ppermute | solution.py:444
  14.3 1.5 %collective-permute-start.3 = (bf16[2,4,2,32,128]{4,3,2,1,0:T(8,128)(2,1)S(1)}, bf16[2,4,2,32,128]{4,3,2,1,0:T(8,128)(2,1)S(1)}, u32[]{:S(2)}, u32[]{:S(2)}) collective-permute-start(bf16[2,4,2,32,128]{4,3,2,1,0:T(8,128)(2,1)S(1)} %get-tuple-element.47), channel_id=1, source_target_pairs={{0,1},{1,0},{2,3},{3,2},{7,6},{6,7},{5,4},{4,5},{8,9},{9,8},{10,11... | collective-permute-start | bytes 393224 | tf_op jit(solution)/shard_map/ppermute | solution.py:519
  15.7 1.5 %collective-permute-start.4 = (bf16[2,4,2,32,128]{4,3,2,1,0:T(8,128)(2,1)S(1)}, bf16[2,4,2,32,128]{4,3,2,1,0:T(8,128)(2,1)S(1)}, u32[]{:S(2)}, u32[]{:S(2)}) collective-permute-start(bf16[2,4,2,32,128]{4,3,2,1,0:T(8,128)(2,1)S(1)} %get-tuple-element.48), channel_id=1, source_target_pairs={{0,4},{1,2},{2,1},{3,7},{7,3},{6,5},{5,6},{4,0},{8,12},{9,10},{10,... | collective-permute-start | bytes 393224 | tf_op jit(solution)/shard_map/ppermute | solution.py:520
  17.2 1.6 %collective-permute-start.6 = (bf16[2,2,4,32,128]{4,3,2,1,0:T(8,128)(2,1)S(1)}, bf16[2,2,4,32,128]{4,3,2,1,0:T(8,128)(2,1)S(1)}, u32[]{:S(2)}, u32[]{:S(2)}) collective-permute-start(bf16[2,2,4,32,128]{4,3,2,1,0:T(8,128)(2,1)S(1)} %get-tuple-element.50), channel_id=1, source_target_pairs={{0,24},{8,16},{16,8},{24,0},{1,25},{9,17},{17,9},{25,1},{2,26},{10... | collective-permute-start | bytes 393224 | tf_op jit(solution)/shard_map/ppermute | solution.py:522
  19.3 1.4 %collective-permute-done.4.yb = bf16[2,4,2,32,128]{4,3,2,1,0:T(8,128)(2,1)S(1)} collective-permute-done((bf16[2,4,2,32,128]{4,3,2,1,0:T(8,128)(2,1)S(1)}, bf16[2,4,2,32,128]{4,3,2,1,0:T(8,128)(2,1)S(1)}, u32[]{:S(2)}, u32[]{:S(2)}) %collective-permute-start.4) | collective-permute-done | bytes 131104 | tf_op jit(solution)/shard_map/ppermute | solution.py:520
  20.8 1.6 %collective-permute-start.9 = (bf16[2,2,4,32,128]{4,3,2,1,0:T(8,128)(2,1)S(1)}, bf16[2,2,4,32,128]{4,3,2,1,0:T(8,128)(2,1)S(1)}, u32[]{:S(2)}, u32[]{:S(2)}) collective-permute-start(bf16[2,2,4,32,128]{4,3,2,1,0:T(8,128)(2,1)S(1)} %get-tuple-element.57), channel_id=1, source_target_pairs={{0,24},{8,16},{16,8},{24,0},{1,25},{9,17},{17,9},{25,1},{2,26},{10... | collective-permute-start | bytes 393224 | tf_op jit(solution)/shard_map/ppermute | solution.py:527
  22.5 1.2 %collective-permute-done.7.other_ref = bf16[32,896]{1,0:T(8,128)(2,1)S(1)} collective-permute-done((bf16[32,896]{1,0:T(8,128)(2,1)S(1)}, bf16[32,896]{1,0:T(8,128)(2,1)S(1)}, u32[]{:S(2)}, u32[]{:S(2)}) %collective-permute-start.7) | collective-permute-done | bytes 57376 | tf_op jit(solution)/shard_map/ppermute | solution.py:523
  24.0 1.8 %shard_map.95 = (bf16[8,8,96,128]{3,2,1,0:T(8,128)(2,1)S(1)}, bf16[8,8,96,128]{3,2,1,0:T(8,128)(2,1)S(1)}, bf16[6,6,96,128]{3,2,1,0:T(8,128)(2,1)S(1)}, bf16[6,6,96,128]{3,2,1,0:T(8,128)(2,1)S(1)}) custom-call(bf16[2,4,4,32,128]{4,3,2,1,0:T(8,128)(2,1)S(1)} %get-tuple-element.46.core, bf16[2,4,2,32,128]{4,3,2,1,0:T(8,128)(2,1)S(1)} %collective-permute-done.3.ya, ...), custom_call_target="tpu_custom_call" | custom-call | flops 264241152 | bytes 5816320 | tf_op jit(solution)/shard_map/pallas_call | solution.py:432
  26.1 3.4 %shard_map.97 = (bf16[4,4,96,128]{3,2,1,0:T(8,128)(2,1)S(1)}, bf16[4,4,96,128]{3,2,1,0:T(8,128)(2,1)S(1)}, f32[32,896]{1,0:T(8,128)S(1)}, f32[32,896]{1,0:T(8,128)S(1)}) custom-call(bf16[2,2,4,32,128]{4,3,2,1,0:T(8,128)(2,1)S(1)} %collective-permute-done.8.ca, bf16[2,2,4,32,128]{4,3,2,1,0:T(8,128)(2,1)S(1)} %collective-permute-done.9.cb, ...), custom_call_target="tpu_custom_call" | custom-call | flops 499122176 | bytes 6307840 | tf_op jit(solution)/shard_map/pallas_call | solution.py:432
  30.0 1.0 %collective-permute-done.13.got_ref = f32[32,896]{1,0:T(8,128)S(1)} collective-permute-done((f32[32,896]{1,0:T(8,128)S(1)}, f32[32,896]{1,0:T(8,128)S(1)}, u32[]{:S(2)}, u32[]{:S(2)}) %collective-permute-start.13) | collective-permute-done | bytes 114720 | tf_op jit(solution)/shard_map/ppermute | solution.py:552
  31.0 0.7 %collective-permute-start.14 = (f32[2,8,896]{2,1,0:T(8,128)S(1)}, f32[2,8,896]{2,1,0:T(8,128)S(1)}, u32[]{:S(2)}, u32[]{:S(2)}) collective-permute-start(f32[2,8,896]{2,1,0:T(8,128)S(1)} %get-tuple-element.73), channel_id=1, source_target_pairs={{0,1},{1,0},{2,3},{3,2},{4,5},{5,4},{6,7},{7,6},{8,9},{9,8},{10,11... | collective-permute-start | bytes 172040 | tf_op jit(solution)/shard_map/ppermute | solution.py:444
  31.7 3.6 %collective-permute-done.14.got_ref = f32[2,8,896]{2,1,0:T(8,128)S(1)} collective-permute-done((f32[2,8,896]{2,1,0:T(8,128)S(1)}, f32[2,8,896]{2,1,0:T(8,128)S(1)}, u32[]{:S(2)}, u32[]{:S(2)}) %collective-permute-start.14) | collective-permute-done | bytes 57376 | tf_op jit(solution)/shard_map/ppermute | solution.py:444
  35.3 1.7 %collective-permute-start.15 = (f32[1,8,896]{2,1,0:T(8,128)S(1)}, f32[1,8,896]{2,1,0:T(8,128)S(1)}, u32[]{:S(2)}, u32[]{:S(2)}) collective-permute-start(f32[1,8,896]{2,1,0:T(8,128)S(1)} %get-tuple-element.75), channel_id=1, source_target_pairs={{0,2},{1,3},{2,0},{3,1},{4,6},{5,7},{6,4},{7,5},{8,10},{9,11},{10,... | collective-permute-start | bytes 86024 | tf_op jit(solution)/shard_map/ppermute | solution.py:444
  36.9 3.5 %collective-permute-done.15.refs_1_ = f32[1,8,896]{2,1,0:T(8,128)S(1)} collective-permute-done((f32[1,8,896]{2,1,0:T(8,128)S(1)}, f32[1,8,896]{2,1,0:T(8,128)S(1)}, u32[]{:S(2)}, u32[]{:S(2)}) %collective-permute-start.15) | collective-permute-done | bytes 28704 | tf_op jit(solution)/shard_map/ppermute | solution.py:444
  40.4 2.4 %collective-permute-start.18 = (f32[1,8,896]{2,1,0:T(8,128)S(1)}, f32[1,8,896]{2,1,0:T(8,128)S(1)}, u32[]{:S(2)}, u32[]{:S(2)}) collective-permute-start(f32[1,8,896]{2,1,0:T(8,128)S(1)} %shard_map.102.refs_0_), channel_id=1, source_target_pairs={{0,20},{4,16},{8,28},{12,24},{16,4},{20,0},{24,12},{28,8},{1,21},{... | collective-permute-start | bytes 86024 | tf_op jit(solution)/shard_map/ppermute | solution.py:589
  42.8 1.3 %shard_map.98 = (bf16[4,2,4,8,128]{4,3,2,1,0:T(8,128)(2,1)S(1)}, bf16[4,2,4,8,128]{4,3,2,1,0:T(8,128)(2,1)S(1)}, bf16[4,2,4,8,128]{4,3,2,1,0:T(8,128)(2,1)S(1)}, bf16[4,2,4,8,128]{4,3,2,1,0:T(8,128)(2,1)S(1)}) custom-call(bf16[6,6,96,128]{3,2,1,0:T(8,128)(2,1)S(1)} %get-tuple-element.54.hid_e, bf16[6,6,96,128]{3,2,1,0:T(8,128)(2,1)S(1)} %get-tuple-element.55.pre_e, ...), custom_call_target="tpu_custom_call" | custom-call | flops 234881024 | bytes 2932736 | tf_op jit(solution)/shard_map/pallas_call | solution.py:432
  44.6 2.6 %collective-permute-start.11 = (bf16[4,2,4,8,128]{4,3,2,1,0:T(8,128)(2,1)S(1)}, bf16[4,2,4,8,128]{4,3,2,1,0:T(8,128)(2,1)S(1)}, u32[]{:S(2)}, u32[]{:S(2)}) collective-permute-start(bf16[4,2,4,8,128]{4,3,2,1,0:T(8,128)(2,1)S(1)} %get-tuple-element.66), channel_id=1, source_target_pairs={{0,2},{1,3},{2,0},{3,1},{4,6},{5,7},{6,4},{7,5},{8,10},{9,11},{10,... | collective-permute-start | bytes 196616 | tf_op jit(solution)/shard_map/ppermute | solution.py:444
  47.3 1.3 %collective-permute-start.12 = (bf16[4,2,4,8,128]{4,3,2,1,0:T(8,128)(2,1)S(1)}, bf16[4,2,4,8,128]{4,3,2,1,0:T(8,128)(2,1)S(1)}, u32[]{:S(2)}, u32[]{:S(2)}) collective-permute-start(bf16[4,2,4,8,128]{4,3,2,1,0:T(8,128)(2,1)S(1)} %get-tuple-element.67), channel_id=1, source_target_pairs={{0,3},{1,2},{2,1},{3,0},{4,7},{5,6},{6,5},{7,4},{8,11},{9,10},{10,... | collective-permute-start | bytes 196616 | tf_op jit(solution)/shard_map/ppermute | solution.py:444
  49.7 2.8 %collective-permute-done.17.refs_2_ = f32[1,8,896]{2,1,0:T(8,128)S(1)} collective-permute-done((f32[1,8,896]{2,1,0:T(8,128)S(1)}, f32[1,8,896]{2,1,0:T(8,128)S(1)}, u32[]{:S(2)}, u32[]{:S(2)}) %collective-permute-start.17) | collective-permute-done | bytes 28704 | tf_op jit(solution)/shard_map/ppermute | solution.py:589
  53.3 0.8 %shard_map.99 = (bf16[8,4,16,128]{3,2,1,0:T(8,128)(2,1)}, bf16[8,4,16,128]{3,2,1,0:T(8,128)(2,1)}) custom-call(bf16[4,2,4,8,128]{4,3,2,1,0:T(8,128)(2,1)S(1)} %get-tuple-element.64.refs_0_, bf16[4,2,4,8,128]{4,3,2,1,0:T(8,128)(2,1)S(1)} %collective-permute-done.10.refs_1_, bf16[4,2,4,8,128]{4,3,2,1,0:T(8,128)(2,1)S(1)} %collective-permute-done.11.refs_2_, ...), custom_call_target="tpu_custom_call" | custom-call | bytes 524288 | tf_op jit(solution)/shard_map/pallas_call | solution.py:432
  54.3 0.8 %shard_map.104 = (f32[27,8,32]{2,1,0:T(8,128)}, f32[27,8,32]{2,1,0:T(8,128)}, f32[1,8]{1,0:T(1,128)}) custom-call(f32[1,8,896]{2,1,0:T(8,128)S(1)} %shard_map.103.own_ref, f32[1,8,896]{2,1,0:T(8,128)S(1)} %collective-permute-done.19.got_ref), custom_call_target="tpu_custom_call" | custom-call | bytes 112672 | tf_op jit(solution)/shard_map/pallas_call | solution.py:432
  (29 shorter events, 4.4 us)
Async XLA Ops:
  1.9 5.7 %collective-permute-start = (bf16[39,8,128]{2,1,0:T(8,128)(2,1)S(1)}, bf16[39,8,128]{2,1,0:T(8,128)(2,1)S(1)}, u32[]{:S(2)}, u32[]{:S(2)}) collective-permute-start(bf16[39,8,128]{2,1,0:T(8,128)(2,1)S(1)} %get-tuple-element.43), channel_id=1, source_target_pairs={{0,1},{1,0},{2,3},{3,2},{4,5},{5,4},{6,7},{7,6},{8,9},{9,8},{10,11... | collective-permute-start | bytes 239624 | tf_op jit(solution)/shard_map/ppermute | solution.py:444
  5.0 9.0 %collective-permute-start.1 = (bf16[39,8,128]{2,1,0:T(8,128)(2,1)S(1)}, bf16[39,8,128]{2,1,0:T(8,128)(2,1)S(1)}, u32[]{:S(2)}, u32[]{:S(2)}) collective-permute-start(bf16[39,8,128]{2,1,0:T(8,128)(2,1)S(1)} %get-tuple-element.44), channel_id=1, source_target_pairs={{0,2},{1,3},{2,0},{3,1},{4,6},{5,7},{6,4},{7,5},{8,10},{9,11},{10,... | collective-permute-start | bytes 239624 | tf_op jit(solution)/shard_map/ppermute | solution.py:444
  7.6 6.5 %collective-permute-start.2 = (bf16[39,8,128]{2,1,0:T(8,128)(2,1)S(1)}, bf16[39,8,128]{2,1,0:T(8,128)(2,1)S(1)}, u32[]{:S(2)}, u32[]{:S(2)}) collective-permute-start(bf16[39,8,128]{2,1,0:T(8,128)(2,1)S(1)} %get-tuple-element.45), channel_id=1, source_target_pairs={{0,3},{1,2},{2,1},{3,0},{4,7},{5,6},{6,5},{7,4},{8,11},{9,10},{10,... | collective-permute-start | bytes 239624 | tf_op jit(solution)/shard_map/ppermute | solution.py:444
  14.3 5.0 %collective-permute-start.3 = (bf16[2,4,2,32,128]{4,3,2,1,0:T(8,128)(2,1)S(1)}, bf16[2,4,2,32,128]{4,3,2,1,0:T(8,128)(2,1)S(1)}, u32[]{:S(2)}, u32[]{:S(2)}) collective-permute-start(bf16[2,4,2,32,128]{4,3,2,1,0:T(8,128)(2,1)S(1)} %get-tuple-element.47), channel_id=1, source_target_pairs={{0,1},{1,0},{2,3},{3,2},{7,6},{6,7},{5,4},{4,5},{8,9},{9,8},{10,11... | collective-permute-start | bytes 393224 | tf_op jit(solution)/shard_map/ppermute | solution.py:519
  15.7 5.0 %collective-permute-start.4 = (bf16[2,4,2,32,128]{4,3,2,1,0:T(8,128)(2,1)S(1)}, bf16[2,4,2,32,128]{4,3,2,1,0:T(8,128)(2,1)S(1)}, u32[]{:S(2)}, u32[]{:S(2)}) collective-permute-start(bf16[2,4,2,32,128]{4,3,2,1,0:T(8,128)(2,1)S(1)} %get-tuple-element.48), channel_id=1, source_target_pairs={{0,4},{1,2},{2,1},{3,7},{7,3},{6,5},{5,6},{4,0},{8,12},{9,10},{10,... | collective-permute-start | bytes 393224 | tf_op jit(solution)/shard_map/ppermute | solution.py:520
  17.2 6.8 %collective-permute-start.5 = (bf16[2,2,4,32,128]{4,3,2,1,0:T(8,128)(2,1)S(1)}, bf16[2,2,4,32,128]{4,3,2,1,0:T(8,128)(2,1)S(1)}, u32[]{:S(2)}, u32[]{:S(2)}) collective-permute-start(bf16[2,2,4,32,128]{4,3,2,1,0:T(8,128)(2,1)S(1)} %get-tuple-element.49), channel_id=1, source_target_pairs={{0,8},{8,0},{16,24},{24,16},{1,9},{9,1},{17,25},{25,17},{2,10},{10... | collective-permute-start | bytes 393224 | tf_op jit(solution)/shard_map/ppermute | solution.py:522
  17.2 6.8 %collective-permute-start.6 = (bf16[2,2,4,32,128]{4,3,2,1,0:T(8,128)(2,1)S(1)}, bf16[2,2,4,32,128]{4,3,2,1,0:T(8,128)(2,1)S(1)}, u32[]{:S(2)}, u32[]{:S(2)}) collective-permute-start(bf16[2,2,4,32,128]{4,3,2,1,0:T(8,128)(2,1)S(1)} %get-tuple-element.50), channel_id=1, source_target_pairs={{0,24},{8,16},{16,8},{24,0},{1,25},{9,17},{17,9},{25,1},{2,26},{10... | collective-permute-start | bytes 393224 | tf_op jit(solution)/shard_map/ppermute | solution.py:522
  20.7 5.1 %collective-permute-start.8 = (bf16[2,2,4,32,128]{4,3,2,1,0:T(8,128)(2,1)S(1)}, bf16[2,2,4,32,128]{4,3,2,1,0:T(8,128)(2,1)S(1)}, u32[]{:S(2)}, u32[]{:S(2)}) collective-permute-start(bf16[2,2,4,32,128]{4,3,2,1,0:T(8,128)(2,1)S(1)} %get-tuple-element.56), channel_id=1, source_target_pairs={{0,8},{8,0},{16,24},{24,16},{1,9},{9,1},{17,25},{25,17},{2,10},{10... | collective-permute-start | bytes 393224 | tf_op jit(solution)/shard_map/ppermute | solution.py:527
  20.8 5.2 %collective-permute-start.9 = (bf16[2,2,4,32,128]{4,3,2,1,0:T(8,128)(2,1)S(1)}, bf16[2,2,4,32,128]{4,3,2,1,0:T(8,128)(2,1)S(1)}, u32[]{:S(2)}, u32[]{:S(2)}) collective-permute-start(bf16[2,2,4,32,128]{4,3,2,1,0:T(8,128)(2,1)S(1)} %get-tuple-element.57), channel_id=1, source_target_pairs={{0,24},{8,16},{16,8},{24,0},{1,25},{9,17},{17,9},{25,1},{2,26},{10... | collective-permute-start | bytes 393224 | tf_op jit(solution)/shard_map/ppermute | solution.py:527
  22.4 1.2 %collective-permute-start.7 = (bf16[32,896]{1,0:T(8,128)(2,1)S(1)}, bf16[32,896]{1,0:T(8,128)(2,1)S(1)}, u32[]{:S(2)}, u32[]{:S(2)}) collective-permute-start(bf16[32,896]{1,0:T(8,128)(2,1)S(1)} %get-tuple-element.51.mine_ref), channel_id=1, source_target_pairs={{0,8},{8,0},{16,24},{24,16},{1,9},{9,1},{17,25},{25,17},{2,10},{10... | collective-permute-start | bytes 172040 | tf_op jit(solution)/shard_map/ppermute | solution.py:523
  29.5 1.5 %collective-permute-start.13 = (f32[32,896]{1,0:T(8,128)S(1)}, f32[32,896]{1,0:T(8,128)S(1)}, u32[]{:S(2)}, u32[]{:S(2)}) collective-permute-start(f32[32,896]{1,0:T(8,128)S(1)} %get-tuple-element.71), channel_id=1, source_target_pairs={{0,8},{8,0},{16,24},{24,16},{1,9},{9,1},{17,25},{25,17},{2,10},{10... | collective-permute-start | bytes 344072 | tf_op jit(solution)/shard_map/ppermute | solution.py:552
  31.0 4.2 %collective-permute-start.14 = (f32[2,8,896]{2,1,0:T(8,128)S(1)}, f32[2,8,896]{2,1,0:T(8,128)S(1)}, u32[]{:S(2)}, u32[]{:S(2)}) collective-permute-start(f32[2,8,896]{2,1,0:T(8,128)S(1)} %get-tuple-element.73), channel_id=1, source_target_pairs={{0,1},{1,0},{2,3},{3,2},{4,5},{5,4},{6,7},{7,6},{8,9},{9,8},{10,11... | collective-permute-start | bytes 172040 | tf_op jit(solution)/shard_map/ppermute | solution.py:444
  35.3 5.1 %collective-permute-start.15 = (f32[1,8,896]{2,1,0:T(8,128)S(1)}, f32[1,8,896]{2,1,0:T(8,128)S(1)}, u32[]{:S(2)}, u32[]{:S(2)}) collective-permute-start(f32[1,8,896]{2,1,0:T(8,128)S(1)} %get-tuple-element.75), channel_id=1, source_target_pairs={{0,2},{1,3},{2,0},{3,1},{4,6},{5,7},{6,4},{7,5},{8,10},{9,11},{10,... | collective-permute-start | bytes 86024 | tf_op jit(solution)/shard_map/ppermute | solution.py:444
  40.4 8.7 %collective-permute-start.18 = (f32[1,8,896]{2,1,0:T(8,128)S(1)}, f32[1,8,896]{2,1,0:T(8,128)S(1)}, u32[]{:S(2)}, u32[]{:S(2)}) collective-permute-start(f32[1,8,896]{2,1,0:T(8,128)S(1)} %shard_map.102.refs_0_), channel_id=1, source_target_pairs={{0,20},{4,16},{8,28},{12,24},{16,4},{20,0},{24,12},{28,8},{1,21},{... | collective-permute-start | bytes 86024 | tf_op jit(solution)/shard_map/ppermute | solution.py:589
  44.2 9.0 %collective-permute-start.10 = (bf16[4,2,4,8,128]{4,3,2,1,0:T(8,128)(2,1)S(1)}, bf16[4,2,4,8,128]{4,3,2,1,0:T(8,128)(2,1)S(1)}, u32[]{:S(2)}, u32[]{:S(2)}) collective-permute-start(bf16[4,2,4,8,128]{4,3,2,1,0:T(8,128)(2,1)S(1)} %get-tuple-element.65), channel_id=1, source_target_pairs={{0,1},{1,0},{2,3},{3,2},{4,5},{5,4},{6,7},{7,6},{8,9},{9,8},{10,11... | collective-permute-start | bytes 196616 | tf_op jit(solution)/shard_map/ppermute | solution.py:444
  44.6 8.5 %collective-permute-start.11 = (bf16[4,2,4,8,128]{4,3,2,1,0:T(8,128)(2,1)S(1)}, bf16[4,2,4,8,128]{4,3,2,1,0:T(8,128)(2,1)S(1)}, u32[]{:S(2)}, u32[]{:S(2)}) collective-permute-start(bf16[4,2,4,8,128]{4,3,2,1,0:T(8,128)(2,1)S(1)} %get-tuple-element.66), channel_id=1, source_target_pairs={{0,2},{1,3},{2,0},{3,1},{4,6},{5,7},{6,4},{7,5},{8,10},{9,11},{10,... | collective-permute-start | bytes 196616 | tf_op jit(solution)/shard_map/ppermute | solution.py:444
  47.3 6.1 %collective-permute-start.12 = (bf16[4,2,4,8,128]{4,3,2,1,0:T(8,128)(2,1)S(1)}, bf16[4,2,4,8,128]{4,3,2,1,0:T(8,128)(2,1)S(1)}, u32[]{:S(2)}, u32[]{:S(2)}) collective-permute-start(bf16[4,2,4,8,128]{4,3,2,1,0:T(8,128)(2,1)S(1)} %get-tuple-element.67), channel_id=1, source_target_pairs={{0,3},{1,2},{2,1},{3,0},{4,7},{5,6},{6,5},{7,4},{8,11},{9,10},{10,... | collective-permute-start | bytes 196616 | tf_op jit(solution)/shard_map/ppermute | solution.py:444
  48.6 3.9 %collective-permute-start.17 = (f32[1,8,896]{2,1,0:T(8,128)S(1)}, f32[1,8,896]{2,1,0:T(8,128)S(1)}, u32[]{:S(2)}, u32[]{:S(2)}) collective-permute-start(f32[1,8,896]{2,1,0:T(8,128)S(1)} %shard_map.102.refs_0_), channel_id=1, source_target_pairs={{0,4},{4,0},{8,12},{12,8},{16,20},{20,16},{24,28},{28,24},{1,5},{5... | collective-permute-start | bytes 86024 | tf_op jit(solution)/shard_map/ppermute | solution.py:589
  49.1 3.9 %collective-permute-start.16 = (f32[1,8,896]{2,1,0:T(8,128)S(1)}, f32[1,8,896]{2,1,0:T(8,128)S(1)}, u32[]{:S(2)}, u32[]{:S(2)}) collective-permute-start(f32[1,8,896]{2,1,0:T(8,128)S(1)} %shard_map.102.refs_0_), channel_id=1, source_target_pairs={{0,16},{4,20},{8,24},{12,28},{16,0},{20,4},{24,8},{28,12},{1,17},{... | collective-permute-start | bytes 86024 | tf_op jit(solution)/shard_map/ppermute | solution.py:589
  53.0 1.3 %collective-permute-start.19 = (f32[1,8,896]{2,1,0:T(8,128)S(1)}, f32[1,8,896]{2,1,0:T(8,128)S(1)}, u32[]{:S(2)}, u32[]{:S(2)}) collective-permute-start(f32[1,8,896]{2,1,0:T(8,128)S(1)} %shard_map.103.own_ref), channel_id=1, source_target_pairs={{0,8},{8,0},{16,24},{24,16},{1,9},{9,1},{17,25},{25,17},{2,10},{10... | collective-permute-start | bytes 86024 | tf_op jit(solution)/shard_map/ppermute | solution.py:593

commit v2 on v1

--- a/solution.py
+++ b/solution.py
@@ -230,15 +230,11 @@
     return lax.dot_general(left, right, (((1,), (1,)), ((), ())), preferred_element_type=F32)
 
 
-def layer(sizes, shape, get_vol, get_cot, one_ref, two_ref, put_hid, put_pre, x, ys, extra):
-    nx, rows, nz = shape
+def activate(sizes, shape, pre_acts, hid_grads, put_hid, put_pre, x, ys):
+    nx, rows = shape
     spot = place(sizes)[3]
     gx = lax.axis_index("gx")
-    pre_acts = dot(one_ref[...], window(get_vol, x, ys, extra))
-    hid_grads = dot(two_ref[...], window(get_cot, x, ys, extra))
-    for n, y in enumerate(ys):
-        at = slice(n * nz, (n + 1) * nz)
-        pre_act = pre_acts[:, at]
+    for pre_act, hid_grad, y in zip(pre_acts, hid_grads, ys):
         sigma = 1.0 / (1.0 + jnp.exp(-pre_act))
         slope = sigma * (1.0 + pre_act * (1.0 - sigma))
         rules = []
@@ -250,19 +246,36 @@
             rules.append(spot > 0)
         if y == rows + 1:
             rules.append(spot < sizes["gy"] * sizes["af"] - 1)
-        for tile, put in ((pre_act * sigma, put_hid), (hid_grads[:, at] * slope, put_pre)):
+        for tile, put in ((pre_act * sigma, put_hid), (hid_grad * slope, put_pre)):
             if rules:
                 ok = functools.reduce(jnp.logical_and, rules)
                 tile = lax.select(ok, tile, jnp.zeros_like(tile))
             put(x, y, tile.astype(BF))
 
 
-def act_body(sizes, core, ya, yb, xa, xb, one_ref, two_ref, vol_s, cot_s, hid_s, pre_s):
+def apart(value, count):
+    size = value.shape[1] // count
+    return [value[:, n * size : (n + 1) * size] for n in range(count)]
+
+
+def row_pairs(nx, rows):
+    for x in range(nx + 2):
+        for start in range(0, rows + 2, 2):
+            late = outside(x, nx - 2, RIM) and outside(start, rows - 2, RIM)
+            yield x, [start, start + 1], late
+
+
+def corner_place(x, size):
+    return x if x < RIM else x - size
+
+
+def act_body(sizes, core, ya, yb, xa, xb, one_ref, two_ref, vol_s, cot_s, hid_s, pre_s, *rest):
     _, nx, rows, width, nz = core.shape
     gx = lax.axis_index("gx")
     y_first, y_second = rim_starts(place(sizes)[3] % 2 == 0, rows)
     x_first, x_second = rim_starts(gx % 2 == 0, nx)
     extra = extra_rows(width, nz)
+    none = jnp.zeros((3 * width, nz), BF)
     for a, stack in enumerate((vol_s, cot_s)):
         for x in range(nx):
             for h in range(RIM):
@@ -276,28 +289,60 @@
                 spread(stack, x_second + h, RIM + y, xb[a, h, y])
 
     def get(stack):
-        return lambda x, y: stack[x, y]
+        def load(x, y):
+            return none if outside(x, nx, RIM) and outside(y, rows, RIM) else stack[x, y]
+
+        return load
 
     def put(stack):
         return lambda x, y, tile: spread(stack, x, y, tile)
 
+    for later in (False, True):
+        for x, ys, late in row_pairs(nx, rows):
+            if late != later:
+                continue
+            sums = [
+                apart(dot(ref[...], window(get(stack), x, ys, extra)), len(ys))
+                for ref, stack in ((one_ref, vol_s), (two_ref, cot_s))
+            ]
+            if not late:
+                activate(sizes, (nx, rows), *sums, put(hid_s), put(pre_s), x, ys)
+                continue
+            for tiles, ref in zip(sums, rest):
+                for y, tile in zip(ys, tiles):
+                    ref[corner_place(x, nx - 2), corner_place(y, rows - 2)] = tile
+
+
+def tap_grad_of(get, center, nx, rows, extra):
+    acc = [None] * 3
     for x in range(nx + 2):
-        for start in range(0, rows + 2, 2):
-            if outside(x, nx - 2, RIM) and outside(start, rows - 2, RIM):
-                continue
-            layer(
-                sizes, (nx, rows, nz), get(vol_s), get(cot_s), one_ref, two_ref,
-                put(hid_s), put(pre_s), x, [start, start + 1], extra,
-            )
+        near = [i for i in range(3) if 0 <= x - i < nx]
+        for start in range(0, rows, 2):
+            ys = [start, start + 1]
+            columns = [
+                jnp.concatenate([get(x, y + j) for j in range(3)] + [extra], axis=0) for y in ys
+            ]
+            left = [
+                jnp.concatenate([center(x - i, y) for y in ys], axis=1) for i in near
+            ]
+            got = dot_cells(jnp.concatenate(left, axis=0), jnp.concatenate(columns, axis=1))
+            size = got.shape[0] // len(near)
+            for n, i in enumerate(near):
+                part = got[n * size : (n + 1) * size]
+                acc[i] = part if acc[i] is None else acc[i] + part
+    width = acc[0].shape[0]
+    return jnp.concatenate(
+        [part[:, : 9 * width] for part in acc] + [acc[0][:, 9 * width :]], axis=1
+    )
 
 
 def fields_body(sizes, ca, cb, one_ref, two_ref, vol_e, cot_e, hid_e, pre_e, *refs):
-    hid_l, pre_l, keep_ref, send_ref, vol_l, cot_l = refs
+    vol_p, cot_p, hid_l, pre_l, keep_ref, send_ref, vol_l, cot_l = refs
     nx, rows = (n - 2 * RIM for n in vol_e.shape[:2])
     width, nz = ca.shape[3:]
-    spot = place(sizes)[3]
     gx = lax.axis_index("gx")
     extra = extra_rows(width, nz)
+    none = jnp.zeros((3 * width, nz), BF)
     x_first, x_second = rim_starts(gx % 2 == 0, 0)
     for a, stack in enumerate((vol_l, cot_l)):
         for h in range(RIM):
@@ -312,36 +357,53 @@
 
     def put(stack):
         def store(x, y, tile):
-            spread(stack, x if x < RIM else x - nx + 2, y if y < RIM else y - rows + 2, tile)
+            spread(stack, corner_place(x, nx - 2), corner_place(y, rows - 2), tile)
 
         return store
 
-    for x in range(nx + 2):
-        for start in range(0, rows + 2, 2):
-            if outside(x, nx - 2, RIM) and outside(start, rows - 2, RIM):
-                layer(
-                    sizes, (nx, rows, nz), get_vol, get_cot, one_ref, two_ref,
-                    put(hid_l), put(pre_l), x, [start, start + 1], extra,
-                )
+    for x, ys, late in row_pairs(nx, rows):
+        if not late:
+            continue
+        far = [i for i in range(3) if outside(x + i, nx, RIM)]
+        js = [j for j in range(3) if any(outside(y + j, rows, RIM) for y in ys)]
+        sums = []
+        for ref, known, get in ((one_ref, vol_p, get_vol), (two_ref, cot_p, get_cot)):
+            left = []
+            for i in far:
+                begin = (3 * i + js[0]) * 3 * width
+                left.append(ref[:, begin : begin + len(js) * 3 * width])
+            columns = []
+            for y in ys:
+                pieces = [
+                    get(x + i, y + j) if outside(y + j, rows, RIM) else none
+                    for i in far
+                    for j in js
+                ]
+                columns.append(jnp.concatenate(pieces, axis=0))
+            got = dot(jnp.concatenate(left, axis=1), jnp.concatenate(columns, axis=1))
+            place_x = corner_place(x, nx - 2)
+            sums.append(
+                [
+                    known[place_x, corner_place(y, rows - 2)] + tile
+                    for y, tile in zip(ys, apart(got, len(ys)))
+                ]
+            )
+        activate(sizes, (nx, rows), *sums, put(hid_l), put(pre_l), x, ys)
 
     middle = slice(width, 2 * width)
-    acc = [None, None]
-    for x in range(nx):
-        ys = list(range(rows))
-        cot = [get_cot(RIM + x, RIM + y, middle) for y in ys]
-        pre = [get_pre(1 + x, 1 + y, middle) for y in ys]
-        got = (
-            dot_cells(jnp.concatenate(cot, axis=1), window(get_hid, x, ys, extra)),
-            dot_cells(
-                jnp.concatenate(pre, axis=1),
-                window(get_vol, x + 1, [y + 1 for y in ys], extra),
-            ),
-        )
-        acc = [g if old is None else old + g for old, g in zip(acc, got)]
-
+    two = tap_grad_of(
+        get_hid, lambda x, y: get_cot(RIM + x, RIM + y, middle), nx, rows, extra
+    )
+    one = tap_grad_of(
+        lambda x, y: get_vol(x + 1, y + 1),
+        lambda x, y: get_pre(1 + x, 1 + y, middle),
+        nx,
+        rows,
+        extra,
+    )
     first_core = gx % 2 == 0
-    keep_ref[...] = lax.select(first_core, acc[0], acc[1])
-    send_ref[...] = lax.select(first_core, acc[1], acc[0])
+    keep_ref[...] = lax.select(first_core, two, one)
+    send_ref[...] = lax.select(first_core, one, two)
 
 
 def split_body(sizes, own_ref, got_ref, keep_ref, send_ref, total):
@@ -393,9 +455,11 @@
         outs[s][...] = turned[me ^ s]
 
 
-def unpack_body(sizes, *refs):
+def finish_body(sizes, scale, taps, width, *refs):
     groups = sizes["af"]
-    parts, (out_ref, grad_ref, flat) = refs[:groups], refs[groups:]
+    parts, totals = refs[:groups], refs[groups : groups + 4]
+    out_ref, grad_ref, one_ref, two_ref, bias_ref, flat = refs[groups + 4 :]
+    total_body(scale, taps, width, *totals, one_ref, two_ref, bias_ref)
     rows, _, nx, chans, _ = parts[0].shape
     ny = rows * groups
     me, row, _, _ = place(sizes)
@@ -412,9 +476,9 @@
                 ref[c, x] = flat[a, x, pl.ds(c, ny, stride=chans), :].astype(BF)
 
 
-def total_body(scale, taps, width, own_ref, got_ref, one_ref, two_ref, bias_ref):
+def total_body(scale, taps, width, own, near, cross, core, one_ref, two_ref, bias_ref):
     first_core = lax.axis_index("gx") % 2 == 0
-    own, got = own_ref[0] * scale, got_ref[0] * scale
+    own, got = (own[0] + near[0]) * scale, (core[0] + cross[0]) * scale
     chans = own.shape[0]
     two, one = lax.select(first_core, own, got), lax.select(first_core, got, own)
     for total, ref in ((one, one_ref), (two, two_ref)):
@@ -532,10 +596,11 @@
     stack = shape((nx + 2 * RIM, rows + 2 * RIM, 3 * width, nz), BF)
     field = shape((nx + 2, rows + 2, 3 * width, nz), BF)
     late = shape((2 * RIM, 2 * RIM, 3 * width, nz), BF)
+    known = shape((2 * RIM, 2 * RIM, width, nz), F32)
     share = shape((width, columns), F32)
     stacks = call(
         bind(act_body, sizes),
-        [stack, stack, field, field],
+        [stack, stack, field, field, known, known],
         [],
         (core, *y_rims, *x_rims, one, two_t),
         flops=2 * width * columns * nz * (nx + 2) * (rows + 2),
@@ -568,46 +633,33 @@
         bind(outputs_body, sizes),
         [piece] * groups,
         [pltpu.VMEM((groups, rows, 2, nx, chans, nz), BF)],
-        (*stacks[2:], hid_l, pre_l, two, one_t),
+        (*stacks[2:4], hid_l, pre_l, two, one_t),
         flops=4 * width * columns * nz * nx * rows,
     )
 
     own = shape((1, chans, columns), F32)
     (total,) = call(sum_body, [own], [], (keep, got))
-    bits = []
-    for axis, low in (("gx", 2), ("gy", 1)):
-        while low < sizes[axis]:
-            bits.append((low if axis == "gy" else low * sizes["gy"]))
-            low *= 2
-    while bits:
-        steps = [0]
-        for bit in bits[:2]:
-            steps += [step ^ bit for step in steps]
-        bits = bits[2:]
-        count = sizes["gx"] * sizes["gy"]
-        got = [
-            lax.ppermute(total, ("gx", "gy"), [(i, i ^ step) for i in range(count)])
-            for step in steps[1:]
-        ]
-        (total,) = call(sum_body, [own], [], [total, *got])
-    last = lax.ppermute(total, "gx", cores)
+    count = sizes["gx"] * sizes["gy"]
+    bits = [1 << n for n in range((count - 1).bit_length())]
+    bits.remove(sizes["gy"])
+    bits.reverse()
+    for bit in bits[:-1]:
+        got = lax.ppermute(total, ("gx", "gy"), [(i, i ^ bit) for i in range(count)])
+        (total,) = call(sum_body, [own], [], (total, got))
+    got = [
+        lax.ppermute(total, ("gx", "gy"), [(i, i ^ step) for i in range(count)])
+        for step in (bits[-1], bits[-1] ^ sizes["gy"], sizes["gy"])
+    ]
 
     pieces = exchange(pieces)
     block = shape((chans, nx, ny, nz), BF)
-    output, input_grad = call(
-        bind(unpack_body, sizes),
-        [block, block],
-        [pltpu.VMEM((2, nx, chans * ny, nz), F32)],
-        pieces,
-    )
-
     cells = nx * sizes["gx"] * ny * sizes["gy"] * nz
     tap_grad = shape((taps, chans, width), F32)
-    grad_one, grad_two, bias_grad = call(
-        bind(total_body, 1.0 / math.sqrt(cells), taps, width),
-        [tap_grad, tap_grad, shape((1, chans), F32)],
-        [],
-        (total, last),
+    output, input_grad, grad_one, grad_two, bias_grad = call(
+        bind(finish_body, sizes, 1.0 / math.sqrt(cells), taps, width),
+        [block, block, tap_grad, tap_grad, shape((1, chans), F32)],
+        [pltpu.VMEM((2, nx, chans * ny, nz), F32)],
+        (*pieces, total, *got),
     )
 
     def unturn(grad):

time: 55.2 us -> 51.9 us (0.940)
  waiting for transfers between devices: 21.4 us -> 19.5 us
  Pallas kernels: 10.1 us -> 9.04 us
    ppermute x8, waiting for transfers between devices: 13.7 us -> 8.59 us  [across(): lax.ppermute(value, 'af', [(i, i ^ step) for i in range(sizes['af'])])]
    ppermute x1, waiting for transfers between devices: 0.17 us -> 3.33 us  [body(): lax.ppermute(total, ('gx', 'gy'), [(i, i ^ bit) for i in range(count)])]
    ppermute x3, starting transfers between devices: 3.49 us -> 2.13 us  [body(): lax.ppermute(total, ('gx', 'gy'), [(i, i ^ step) for i in range(count)])]
    pallas_call x13 -> x12, Pallas kernels: 10.1 us -> 9.04 us  [call(): pl.pallas_call(body, out_shape=tuple(outs), in_specs=specs or [pl.BlockSp...]
    ppermute x8, starting transfers between devices: 12.5 us -> 13.3 us  [across(): lax.ppermute(value, 'af', [(i, i ^ step) for i in range(sizes['af'])])]
  transfers between devices with their start and end apart: 20 -> 20, of which waited for: 12 -> 10; matrix products, arithmetic and copies ran while one was open for 0% -> 0% of each run, Pallas kernels for 8% -> 9%
where the time goes in v2:
time: 51.9 us; the launch traced here: 51.8 us
  starting transfers between devices  22.5 us (43%)
  waiting for transfers between devices  19.5 us (38%)
  Pallas kernels  9.04 us (17%)
  between operations  0.74 us (1%)
    ppermute x8, starting transfers between devices, across(): lax.ppermute(value, 'af', [(i, i ^ step) for i in range(sizes['af'])])  13.3 us
    pallas_call x12, Pallas kernels, call(): pl.pallas_call(body, out_shape=tuple(outs), in_specs=specs or [pl.BlockSp...  9.04 us
    ppermute x8, waiting for transfers between devices, across(): lax.ppermute(value, 'af', [(i, i ^ step) for i in range(sizes['af'])])  8.59 us
    ppermute x1, waiting for transfers between devices, body(): lax.ppermute(total, ('gx', 'gy'), [(i, i ^ bit) for i in range(count)])  3.33 us
    ppermute x3, waiting for transfers between devices, body(): lax.ppermute(total, ('gx', 'gy'), [(i, i ^ step) for i in range(count)])  3.32 us
    ppermute x3, starting transfers between devices, body(): lax.ppermute(total, ('gx', 'gy'), [(i, i ^ step) for i in range(count)])  2.13 us
    ppermute x2, starting transfers between devices, body(): corners = (lax.ppermute(c_one, 'gx', near), lax.ppermute(c_two, 'gx', wrap))  1.66 us
    ppermute x2, starting transfers between devices, body(): x_rims = (lax.ppermute(x_one, 'gx', near), lax.ppermute(x_two, 'gx', wrap))  1.62 us
  transfers between devices with their start and end apart: 20, of which 10 were waited for; matrix products, arithmetic and copies ran while one was open for 0% of the time, Pallas kernels for 9%

profile of v2, /device:TPU:0, one launch (start us, length us, event | category | flops | bytes accessed | tf_op | source)
XLA Modules:
  0.0 51.8 jit_solution(7917753945895856311)
XLA Ops:
  0.6 1.3 %shard_map.92 = (bf16[39,8,128]{2,1,0:T(8,128)(2,1)S(1)}, bf16[39,8,128]{2,1,0:T(8,128)(2,1)S(1)}, bf16[39,8,128]{2,1,0:T(8,128)(2,1)S(1)}, bf16[39,8,128]{2,1,0:T(8,128)(2,1)S(1)}) custom-call(bf16[8,4,16,128]{3,2,1,0:T(8,128)(2,1)} %vol_hbm.1, bf16[8,4,16,128]{3,2,1,0:T(8,128)(2,1)} %cot_hbm.1, bf16[27,8,32]{2,1,0:T(8,128)(2,1)} %bitcast.14, ...), custom_call_target="tpu_custom_call" | custom-call | bytes 609312 | tf_op jit(solution)/shard_map/pallas_call | solution.py:496
  1.9 3.1 %collective-permute-start = (bf16[39,8,128]{2,1,0:T(8,128)(2,1)S(1)}, bf16[39,8,128]{2,1,0:T(8,128)(2,1)S(1)}, u32[]{:S(2)}, u32[]{:S(2)}) collective-permute-start(bf16[39,8,128]{2,1,0:T(8,128)(2,1)S(1)} %get-tuple-element.45), channel_id=1, source_target_pairs={{0,1},{1,0},{2,3},{3,2},{4,5},{5,4},{6,7},{7,6},{8,9},{9,8},{10,11... | collective-permute-start | bytes 239624 | tf_op jit(solution)/shard_map/ppermute | solution.py:508
  5.0 2.6 %collective-permute-start.1 = (bf16[39,8,128]{2,1,0:T(8,128)(2,1)S(1)}, bf16[39,8,128]{2,1,0:T(8,128)(2,1)S(1)}, u32[]{:S(2)}, u32[]{:S(2)}) collective-permute-start(bf16[39,8,128]{2,1,0:T(8,128)(2,1)S(1)} %get-tuple-element.46), channel_id=1, source_target_pairs={{0,2},{1,3},{2,0},{3,1},{4,6},{5,7},{6,4},{7,5},{8,10},{9,11},{10,... | collective-permute-start | bytes 239624 | tf_op jit(solution)/shard_map/ppermute | solution.py:508
  7.6 6.4 %collective-permute-done.1.refs_2_ = bf16[39,8,128]{2,1,0:T(8,128)(2,1)S(1)} collective-permute-done((bf16[39,8,128]{2,1,0:T(8,128)(2,1)S(1)}, bf16[39,8,128]{2,1,0:T(8,128)(2,1)S(1)}, u32[]{:S(2)}, u32[]{:S(2)}) %collective-permute-start.1) | collective-permute-done | bytes 79904 | tf_op jit(solution)/shard_map/ppermute | solution.py:508
  14.3 1.5 %collective-permute-start.3 = (bf16[2,4,2,32,128]{4,3,2,1,0:T(8,128)(2,1)S(1)}, bf16[2,4,2,32,128]{4,3,2,1,0:T(8,128)(2,1)S(1)}, u32[]{:S(2)}, u32[]{:S(2)}) collective-permute-start(bf16[2,4,2,32,128]{4,3,2,1,0:T(8,128)(2,1)S(1)} %get-tuple-element.49), channel_id=1, source_target_pairs={{0,1},{1,0},{2,3},{3,2},{7,6},{6,7},{5,4},{4,5},{8,9},{9,8},{10,11... | collective-permute-start | bytes 393224 | tf_op jit(solution)/shard_map/ppermute | solution.py:583
  15.7 1.5 %collective-permute-start.4 = (bf16[2,4,2,32,128]{4,3,2,1,0:T(8,128)(2,1)S(1)}, bf16[2,4,2,32,128]{4,3,2,1,0:T(8,128)(2,1)S(1)}, u32[]{:S(2)}, u32[]{:S(2)}) collective-permute-start(bf16[2,4,2,32,128]{4,3,2,1,0:T(8,128)(2,1)S(1)} %get-tuple-element.50), channel_id=1, source_target_pairs={{0,4},{1,2},{2,1},{3,7},{7,3},{6,5},{5,6},{4,0},{8,12},{9,10},{10,... | collective-permute-start | bytes 393224 | tf_op jit(solution)/shard_map/ppermute | solution.py:584
  17.2 1.6 %collective-permute-start.6 = (bf16[2,2,4,32,128]{4,3,2,1,0:T(8,128)(2,1)S(1)}, bf16[2,2,4,32,128]{4,3,2,1,0:T(8,128)(2,1)S(1)}, u32[]{:S(2)}, u32[]{:S(2)}) collective-permute-start(bf16[2,2,4,32,128]{4,3,2,1,0:T(8,128)(2,1)S(1)} %get-tuple-element.52), channel_id=1, source_target_pairs={{0,24},{8,16},{16,8},{24,0},{1,25},{9,17},{17,9},{25,1},{2,26},{10... | collective-permute-start | bytes 393224 | tf_op jit(solution)/shard_map/ppermute | solution.py:586
  19.3 1.4 %collective-permute-done.4.yb = bf16[2,4,2,32,128]{4,3,2,1,0:T(8,128)(2,1)S(1)} collective-permute-done((bf16[2,4,2,32,128]{4,3,2,1,0:T(8,128)(2,1)S(1)}, bf16[2,4,2,32,128]{4,3,2,1,0:T(8,128)(2,1)S(1)}, u32[]{:S(2)}, u32[]{:S(2)}) %collective-permute-start.4) | collective-permute-done | bytes 131104 | tf_op jit(solution)/shard_map/ppermute | solution.py:584
  20.8 1.6 %collective-permute-start.9 = (bf16[2,2,4,32,128]{4,3,2,1,0:T(8,128)(2,1)S(1)}, bf16[2,2,4,32,128]{4,3,2,1,0:T(8,128)(2,1)S(1)}, u32[]{:S(2)}, u32[]{:S(2)}) collective-permute-start(bf16[2,2,4,32,128]{4,3,2,1,0:T(8,128)(2,1)S(1)} %get-tuple-element.59), channel_id=1, source_target_pairs={{0,24},{8,16},{16,8},{24,0},{1,25},{9,17},{17,9},{25,1},{2,26},{10... | collective-permute-start | bytes 393224 | tf_op jit(solution)/shard_map/ppermute | solution.py:591
  22.5 1.2 %collective-permute-done.7.other_ref = bf16[32,896]{1,0:T(8,128)(2,1)S(1)} collective-permute-done((bf16[32,896]{1,0:T(8,128)(2,1)S(1)}, bf16[32,896]{1,0:T(8,128)(2,1)S(1)}, u32[]{:S(2)}, u32[]{:S(2)}) %collective-permute-start.7) | collective-permute-done | bytes 57376 | tf_op jit(solution)/shard_map/ppermute | solution.py:587
  24.0 3.1 %shard_map.95 = (bf16[8,8,96,128]{3,2,1,0:T(8,128)(2,1)S(1)}, bf16[8,8,96,128]{3,2,1,0:T(8,128)(2,1)S(1)}, bf16[6,6,96,128]{3,2,1,0:T(8,128)(2,1)S(1)}, bf16[6,6...) custom-call(bf16[2,4,4,32,128]{4,3,2,1,0:T(8,128)(2,1)S(1)} %get-tuple-element.48.core, ...), custom_call_target="tpu_custom_call" | custom-call | flops 264241152 | bytes 6340608 | tf_op jit(solution)/shard_map/pallas_call | solution.py:496
  27.1 1.9 %shard_map.97 = (bf16[4,4,96,128]{3,2,1,0:T(8,128)(2,1)S(1)}, bf16[4,4,96,128]{3,2,1,0:T(8,128)(2,1)S(1)}, f32[32,896]{1,0:T(8,128)S(1)}, f32[32,896]{1,0:T(8,128)S(1)}) custom-call(bf16[2,2,4,32,128]{4,3,2,1,0:T(8,128)(2,1)S(1)} %collective-permute-done.8.ca, bf16[2,2,4,32,128]{4,3,2,1,0:T(8,128)(2,1)S(1)} %collective-permute-done.9.cb, ...), custom_call_target="tpu_custom_call" | custom-call | flops 499122176 | bytes 6832128 | tf_op jit(solution)/shard_map/pallas_call | solution.py:496
  29.2 1.2 %collective-permute-done.13.got_ref = f32[32,896]{1,0:T(8,128)S(1)} collective-permute-done((f32[32,896]{1,0:T(8,128)S(1)}, f32[32,896]{1,0:T(8,128)S(1)}, u32[]{:S(2)}, u32[]{:S(2)}) %collective-permute-start.13) | collective-permute-done | bytes 114720 | tf_op jit(solution)/shard_map/ppermute | solution.py:617
  31.1 1.3 %shard_map.98 = (bf16[4,2,4,8,128]{4,3,2,1,0:T(8,128)(2,1)S(1)}, bf16[4,2,4,8,128]{4,3,2,1,0:T(8,128)(2,1)S(1)}, bf16[4,2,4,8,128]{4,3,2,1,0:T(8,128)(2,1)S(1)}, bf16[4,2,4,8,128]{4,3,2,1,0:T(8,128)(2,1)S(1)}) custom-call(bf16[6,6,96,128]{3,2,1,0:T(8,128)(2,1)S(1)} %get-tuple-element.56.hid_e, bf16[6,6,96,128]{3,2,1,0:T(8,128)(2,1)S(1)} %get-tuple-element.57.pre_e, ...), custom_call_target="tpu_custom_call" | custom-call | flops 234881024 | bytes 2932736 | tf_op jit(solution)/shard_map/pallas_call | solution.py:496
  32.4 1.5 %collective-permute-start.10 = (bf16[4,2,4,8,128]{4,3,2,1,0:T(8,128)(2,1)S(1)}, bf16[4,2,4,8,128]{4,3,2,1,0:T(8,128)(2,1)S(1)}, u32[]{:S(2)}, u32[]{:S(2)}) collective-permute-start(bf16[4,2,4,8,128]{4,3,2,1,0:T(8,128)(2,1)S(1)} %get-tuple-element.69), channel_id=1, source_target_pairs={{0,1},{1,0},{2,3},{3,2},{4,5},{5,4},{6,7},{7,6},{8,9},{9,8},{10,11... | collective-permute-start | bytes 196616 | tf_op jit(solution)/shard_map/ppermute | solution.py:508
  34.7 1.7 %collective-permute-start.15 = (f32[1,8,896]{2,1,0:T(8,128)S(1)}, f32[1,8,896]{2,1,0:T(8,128)S(1)}, u32[]{:S(2)}, u32[]{:S(2)}) collective-permute-start(f32[1,8,896]{2,1,0:T(8,128)S(1)} %get-tuple-element.77), channel_id=1, source_target_pairs={{0,2},{1,3},{2,0},{3,1},{4,6},{5,7},{6,4},{7,5},{8,10},{9,11},{10,... | collective-permute-start | bytes 86024 | tf_op jit(solution)/shard_map/ppermute | solution.py:508
  36.4 1.3 %collective-permute-start.11 = (bf16[4,2,4,8,128]{4,3,2,1,0:T(8,128)(2,1)S(1)}, bf16[4,2,4,8,128]{4,3,2,1,0:T(8,128)(2,1)S(1)}, u32[]{:S(2)}, u32[]{:S(2)}) collective-permute-start(bf16[4,2,4,8,128]{4,3,2,1,0:T(8,128)(2,1)S(1)} %get-tuple-element.70), channel_id=1, source_target_pairs={{0,2},{1,3},{2,0},{3,1},{4,6},{5,7},{6,4},{7,5},{8,10},{9,11},{10,... | collective-permute-start | bytes 196616 | tf_op jit(solution)/shard_map/ppermute | solution.py:508
  37.7 2.5 %collective-permute-start.12 = (bf16[4,2,4,8,128]{4,3,2,1,0:T(8,128)(2,1)S(1)}, bf16[4,2,4,8,128]{4,3,2,1,0:T(8,128)(2,1)S(1)}, u32[]{:S(2)}, u32[]{:S(2)}) collective-permute-start(bf16[4,2,4,8,128]{4,3,2,1,0:T(8,128)(2,1)S(1)} %get-tuple-element.71), channel_id=1, source_target_pairs={{0,3},{1,2},{2,1},{3,0},{4,7},{5,6},{6,5},{7,4},{8,11},{9,10},{10,... | collective-permute-start | bytes 196616 | tf_op jit(solution)/shard_map/ppermute | solution.py:508
  40.1 1.4 %collective-permute-done.15.refs_1_ = f32[1,8,896]{2,1,0:T(8,128)S(1)} collective-permute-done((f32[1,8,896]{2,1,0:T(8,128)S(1)}, f32[1,8,896]{2,1,0:T(8,128)S(1)}, u32[]{:S(2)}, u32[]{:S(2)}) %collective-permute-start.15) | collective-permute-done | bytes 28704 | tf_op jit(solution)/shard_map/ppermute | solution.py:508
  42.1 3.3 %collective-permute-done.16.refs_1_ = f32[1,8,896]{2,1,0:T(8,128)S(1)} collective-permute-done((f32[1,8,896]{2,1,0:T(8,128)S(1)}, f32[1,8,896]{2,1,0:T(8,128)S(1)}, u32[]{:S(2)}, u32[]{:S(2)}) %collective-permute-start.16) | collective-permute-done | bytes 28704 | tf_op jit(solution)/shard_map/ppermute | solution.py:647
  45.4 1.6 %collective-permute-start.18 = (f32[1,8,896]{2,1,0:T(8,128)S(1)}, f32[1,8,896]{2,1,0:T(8,128)S(1)}, u32[]{:S(2)}, u32[]{:S(2)}) collective-permute-start(f32[1,8,896]{2,1,0:T(8,128)S(1)} %shard_map.102.refs_4_), channel_id=1, source_target_pairs={{0,12},{4,8},{8,4},{12,0},{16,28},{20,24},{24,20},{28,16},{1,13},{... | collective-permute-start | bytes 86024 | tf_op jit(solution)/shard_map/ppermute | solution.py:650
  47.6 1.2 %collective-permute-done.18.refs_6_ = f32[1,8,896]{2,1,0:T(8,128)S(1)} collective-permute-done((f32[1,8,896]{2,1,0:T(8,128)S(1)}, f32[1,8,896]{2,1,0:T(8,128)S(1)}, u32[]{:S(2)}, u32[]{:S(2)}) %collective-permute-start.18) | collective-permute-done | bytes 28704 | tf_op jit(solution)/shard_map/ppermute | solution.py:650
  48.8 2.1 %collective-permute-done.17.refs_5_ = f32[1,8,896]{2,1,0:T(8,128)S(1)} collective-permute-done((f32[1,8,896]{2,1,0:T(8,128)S(1)}, f32[1,8,896]{2,1,0:T(8,128)S(1)}, u32[]{:S(2)}, u32[]{:S(2)}) %collective-permute-start.17) | collective-permute-done | bytes 28704 | tf_op jit(solution)/shard_map/ppermute | solution.py:650
  50.9 0.9 %shard_map.103 = (bf16[8,4,16,128]{3,2,1,0:T(8,128)(2,1)}, bf16[8,4,16,128]{3,2,1,0:T(8,128)(2,1)}, f32[27,8,32]{2,1,0:T(8,128)}, f32[27,8,32]{2,1,0:T(8,128)}, f32[1,8]{1,0:T(1,128)}) custom-call(bf16[4,2,4,8,128]{4,3,2,1,0:T(8,128)(2,1)S(1)} %get-tuple-element.68.refs_0_, bf16[4,2,4,8,128]{4,3,2,1,0:T(8,128)(2,1)S(1)} %collective-permute-done.10.refs_1_, ...), custom_call_target="tpu_custom_call" | custom-call | bytes 694304 | tf_op jit(solution)/shard_map/pallas_call | solution.py:496
  (28 shorter events, 3.9 us)
Async XLA Ops:
  1.9 5.7 %collective-permute-start = (bf16[39,8,128]{2,1,0:T(8,128)(2,1)S(1)}, bf16[39,8,128]{2,1,0:T(8,128)(2,1)S(1)}, u32[]{:S(2)}, u32[]{:S(2)}) collective-permute-start(bf16[39,8,128]{2,1,0:T(8,128)(2,1)S(1)} %get-tuple-element.45), channel_id=1, source_target_pairs={{0,1},{1,0},{2,3},{3,2},{4,5},{5,4},{6,7},{7,6},{8,9},{9,8},{10,11... | collective-permute-start | bytes 239624 | tf_op jit(solution)/shard_map/ppermute | solution.py:508
  5.0 9.0 %collective-permute-start.1 = (bf16[39,8,128]{2,1,0:T(8,128)(2,1)S(1)}, bf16[39,8,128]{2,1,0:T(8,128)(2,1)S(1)}, u32[]{:S(2)}, u32[]{:S(2)}) collective-permute-start(bf16[39,8,128]{2,1,0:T(8,128)(2,1)S(1)} %get-tuple-element.46), channel_id=1, source_target_pairs={{0,2},{1,3},{2,0},{3,1},{4,6},{5,7},{6,4},{7,5},{8,10},{9,11},{10,... | collective-permute-start | bytes 239624 | tf_op jit(solution)/shard_map/ppermute | solution.py:508
  7.6 6.5 %collective-permute-start.2 = (bf16[39,8,128]{2,1,0:T(8,128)(2,1)S(1)}, bf16[39,8,128]{2,1,0:T(8,128)(2,1)S(1)}, u32[]{:S(2)}, u32[]{:S(2)}) collective-permute-start(bf16[39,8,128]{2,1,0:T(8,128)(2,1)S(1)} %get-tuple-element.47), channel_id=1, source_target_pairs={{0,3},{1,2},{2,1},{3,0},{4,7},{5,6},{6,5},{7,4},{8,11},{9,10},{10,... | collective-permute-start | bytes 239624 | tf_op jit(solution)/shard_map/ppermute | solution.py:508
  14.3 5.0 %collective-permute-start.3 = (bf16[2,4,2,32,128]{4,3,2,1,0:T(8,128)(2,1)S(1)}, bf16[2,4,2,32,128]{4,3,2,1,0:T(8,128)(2,1)S(1)}, u32[]{:S(2)}, u32[]{:S(2)}) collective-permute-start(bf16[2,4,2,32,128]{4,3,2,1,0:T(8,128)(2,1)S(1)} %get-tuple-element.49), channel_id=1, source_target_pairs={{0,1},{1,0},{2,3},{3,2},{7,6},{6,7},{5,4},{4,5},{8,9},{9,8},{10,11... | collective-permute-start | bytes 393224 | tf_op jit(solution)/shard_map/ppermute | solution.py:583
  15.7 5.0 %collective-permute-start.4 = (bf16[2,4,2,32,128]{4,3,2,1,0:T(8,128)(2,1)S(1)}, bf16[2,4,2,32,128]{4,3,2,1,0:T(8,128)(2,1)S(1)}, u32[]{:S(2)}, u32[]{:S(2)}) collective-permute-start(bf16[2,4,2,32,128]{4,3,2,1,0:T(8,128)(2,1)S(1)} %get-tuple-element.50), channel_id=1, source_target_pairs={{0,4},{1,2},{2,1},{3,7},{7,3},{6,5},{5,6},{4,0},{8,12},{9,10},{10,... | collective-permute-start | bytes 393224 | tf_op jit(solution)/shard_map/ppermute | solution.py:584
  17.2 6.8 %collective-permute-start.5 = (bf16[2,2,4,32,128]{4,3,2,1,0:T(8,128)(2,1)S(1)}, bf16[2,2,4,32,128]{4,3,2,1,0:T(8,128)(2,1)S(1)}, u32[]{:S(2)}, u32[]{:S(2)}) collective-permute-start(bf16[2,2,4,32,128]{4,3,2,1,0:T(8,128)(2,1)S(1)} %get-tuple-element.51), channel_id=1, source_target_pairs={{0,8},{8,0},{16,24},{24,16},{1,9},{9,1},{17,25},{25,17},{2,10},{10... | collective-permute-start | bytes 393224 | tf_op jit(solution)/shard_map/ppermute | solution.py:586
  17.2 6.8 %collective-permute-start.6 = (bf16[2,2,4,32,128]{4,3,2,1,0:T(8,128)(2,1)S(1)}, bf16[2,2,4,32,128]{4,3,2,1,0:T(8,128)(2,1)S(1)}, u32[]{:S(2)}, u32[]{:S(2)}) collective-permute-start(bf16[2,2,4,32,128]{4,3,2,1,0:T(8,128)(2,1)S(1)} %get-tuple-element.52), channel_id=1, source_target_pairs={{0,24},{8,16},{16,8},{24,0},{1,25},{9,17},{17,9},{25,1},{2,26},{10... | collective-permute-start | bytes 393224 | tf_op jit(solution)/shard_map/ppermute | solution.py:586
  20.7 6.3 %collective-permute-start.8 = (bf16[2,2,4,32,128]{4,3,2,1,0:T(8,128)(2,1)S(1)}, bf16[2,2,4,32,128]{4,3,2,1,0:T(8,128)(2,1)S(1)}, u32[]{:S(2)}, u32[]{:S(2)}) collective-permute-start(bf16[2,2,4,32,128]{4,3,2,1,0:T(8,128)(2,1)S(1)} %get-tuple-element.58), channel_id=1, source_target_pairs={{0,8},{8,0},{16,24},{24,16},{1,9},{9,1},{17,25},{25,17},{2,10},{10... | collective-permute-start | bytes 393224 | tf_op jit(solution)/shard_map/ppermute | solution.py:591
  20.8 6.3 %collective-permute-start.9 = (bf16[2,2,4,32,128]{4,3,2,1,0:T(8,128)(2,1)S(1)}, bf16[2,2,4,32,128]{4,3,2,1,0:T(8,128)(2,1)S(1)}, u32[]{:S(2)}, u32[]{:S(2)}) collective-permute-start(bf16[2,2,4,32,128]{4,3,2,1,0:T(8,128)(2,1)S(1)} %get-tuple-element.59), channel_id=1, source_target_pairs={{0,24},{8,16},{16,8},{24,0},{1,25},{9,17},{17,9},{25,1},{2,26},{10... | collective-permute-start | bytes 393224 | tf_op jit(solution)/shard_map/ppermute | solution.py:591
  22.4 1.2 %collective-permute-start.7 = (bf16[32,896]{1,0:T(8,128)(2,1)S(1)}, bf16[32,896]{1,0:T(8,128)(2,1)S(1)}, u32[]{:S(2)}, u32[]{:S(2)}) collective-permute-start(bf16[32,896]{1,0:T(8,128)(2,1)S(1)} %get-tuple-element.53.mine_ref), channel_id=1, source_target_pairs={{0,8},{8,0},{16,24},{24,16},{1,9},{9,1},{17,25},{25,17},{2,10},{10... | collective-permute-start | bytes 172040 | tf_op jit(solution)/shard_map/ppermute | solution.py:587
  29.0 1.4 %collective-permute-start.13 = (f32[32,896]{1,0:T(8,128)S(1)}, f32[32,896]{1,0:T(8,128)S(1)}, u32[]{:S(2)}, u32[]{:S(2)}) collective-permute-start(f32[32,896]{1,0:T(8,128)S(1)} %get-tuple-element.73), channel_id=1, source_target_pairs={{0,8},{8,0},{16,24},{24,16},{1,9},{9,1},{17,25},{25,17},{2,10},{10... | collective-permute-start | bytes 344072 | tf_op jit(solution)/shard_map/ppermute | solution.py:617
  30.4 4.2 %collective-permute-start.14 = (f32[2,8,896]{2,1,0:T(8,128)S(1)}, f32[2,8,896]{2,1,0:T(8,128)S(1)}, u32[]{:S(2)}, u32[]{:S(2)}) collective-permute-start(f32[2,8,896]{2,1,0:T(8,128)S(1)} %get-tuple-element.75), channel_id=1, source_target_pairs={{0,1},{1,0},{2,3},{3,2},{4,5},{5,4},{6,7},{7,6},{8,9},{9,8},{10,11... | collective-permute-start | bytes 172040 | tf_op jit(solution)/shard_map/ppermute | solution.py:508
  32.4 14.6 %collective-permute-start.10 = (bf16[4,2,4,8,128]{4,3,2,1,0:T(8,128)(2,1)S(1)}, bf16[4,2,4,8,128]{4,3,2,1,0:T(8,128)(2,1)S(1)}, u32[]{:S(2)}, u32[]{:S(2)}) collective-permute-start(bf16[4,2,4,8,128]{4,3,2,1,0:T(8,128)(2,1)S(1)} %get-tuple-element.69), channel_id=1, source_target_pairs={{0,1},{1,0},{2,3},{3,2},{4,5},{5,4},{6,7},{7,6},{8,9},{9,8},{10,11... | collective-permute-start | bytes 196616 | tf_op jit(solution)/shard_map/ppermute | solution.py:508
  34.7 6.9 %collective-permute-start.15 = (f32[1,8,896]{2,1,0:T(8,128)S(1)}, f32[1,8,896]{2,1,0:T(8,128)S(1)}, u32[]{:S(2)}, u32[]{:S(2)}) collective-permute-start(f32[1,8,896]{2,1,0:T(8,128)S(1)} %get-tuple-element.77), channel_id=1, source_target_pairs={{0,2},{1,3},{2,0},{3,1},{4,6},{5,7},{6,4},{7,5},{8,10},{9,11},{10,... | collective-permute-start | bytes 86024 | tf_op jit(solution)/shard_map/ppermute | solution.py:508
  36.4 11.2 %collective-permute-start.11 = (bf16[4,2,4,8,128]{4,3,2,1,0:T(8,128)(2,1)S(1)}, bf16[4,2,4,8,128]{4,3,2,1,0:T(8,128)(2,1)S(1)}, u32[]{:S(2)}, u32[]{:S(2)}) collective-permute-start(bf16[4,2,4,8,128]{4,3,2,1,0:T(8,128)(2,1)S(1)} %get-tuple-element.70), channel_id=1, source_target_pairs={{0,2},{1,3},{2,0},{3,1},{4,6},{5,7},{6,4},{7,5},{8,10},{9,11},{10,... | collective-permute-start | bytes 196616 | tf_op jit(solution)/shard_map/ppermute | solution.py:508
  37.7 9.9 %collective-permute-start.12 = (bf16[4,2,4,8,128]{4,3,2,1,0:T(8,128)(2,1)S(1)}, bf16[4,2,4,8,128]{4,3,2,1,0:T(8,128)(2,1)S(1)}, u32[]{:S(2)}, u32[]{:S(2)}) collective-permute-start(bf16[4,2,4,8,128]{4,3,2,1,0:T(8,128)(2,1)S(1)} %get-tuple-element.71), channel_id=1, source_target_pairs={{0,3},{1,2},{2,1},{3,0},{4,7},{5,6},{6,5},{7,4},{8,11},{9,10},{10,... | collective-permute-start | bytes 196616 | tf_op jit(solution)/shard_map/ppermute | solution.py:508
  41.5 3.9 %collective-permute-start.16 = (f32[1,8,896]{2,1,0:T(8,128)S(1)}, f32[1,8,896]{2,1,0:T(8,128)S(1)}, u32[]{:S(2)}, u32[]{:S(2)}) collective-permute-start(f32[1,8,896]{2,1,0:T(8,128)S(1)} %shard_map.101.refs_0_), channel_id=1, source_target_pairs={{0,16},{4,20},{8,24},{12,28},{16,0},{20,4},{24,8},{28,12},{1,17},{... | collective-permute-start | bytes 86024 | tf_op jit(solution)/shard_map/ppermute | solution.py:647
  45.4 2.2 %collective-permute-start.19 = (f32[1,8,896]{2,1,0:T(8,128)S(1)}, f32[1,8,896]{2,1,0:T(8,128)S(1)}, u32[]{:S(2)}, u32[]{:S(2)}) collective-permute-start(f32[1,8,896]{2,1,0:T(8,128)S(1)} %shard_map.102.refs_4_), channel_id=1, source_target_pairs={{0,8},{4,12},{8,0},{12,4},{16,24},{20,28},{24,16},{28,20},{1,9},{5... | collective-permute-start | bytes 86024 | tf_op jit(solution)/shard_map/ppermute | solution.py:650
  45.4 3.4 %collective-permute-start.18 = (f32[1,8,896]{2,1,0:T(8,128)S(1)}, f32[1,8,896]{2,1,0:T(8,128)S(1)}, u32[]{:S(2)}, u32[]{:S(2)}) collective-permute-start(f32[1,8,896]{2,1,0:T(8,128)S(1)} %shard_map.102.refs_4_), channel_id=1, source_target_pairs={{0,12},{4,8},{8,4},{12,0},{16,28},{20,24},{24,20},{28,16},{1,13},{... | collective-permute-start | bytes 86024 | tf_op jit(solution)/shard_map/ppermute | solution.py:650
  47.0 3.9 %collective-permute-start.17 = (f32[1,8,896]{2,1,0:T(8,128)S(1)}, f32[1,8,896]{2,1,0:T(8,128)S(1)}, u32[]{:S(2)}, u32[]{:S(2)}) collective-permute-start(f32[1,8,896]{2,1,0:T(8,128)S(1)} %shard_map.102.refs_4_), channel_id=1, source_target_pairs={{0,4},{4,0},{8,12},{12,8},{16,20},{20,16},{24,28},{28,24},{1,5},{5... | collective-permute-start | bytes 86024 | tf_op jit(solution)/shard_map/ppermute | solution.py:650

commit v3 on v2

--- a/solution.py
+++ b/solution.py
@@ -11,6 +11,7 @@
 
 BF = jnp.bfloat16
 F32 = jnp.float32
+ALL = ("gx", "gy", "af")
 LIMIT = 20 << 20
 RIM = 2
 
@@ -621,13 +622,23 @@
         [pltpu.VMEM((groups, chans, columns), F32)],
         (keep, got),
     )
+    count = sizes["gx"] * sizes["gy"]
+    bits = [1 << n for n in range((count - 1).bit_length())]
+    bits.remove(sizes["gy"])
+    bits.reverse()
     bit = 1
-    while bit < groups:
+    while 2 * bit < groups:
         got = across(send, bit, sizes)
-        if 2 * bit < groups:
-            half = shape((groups // (4 * bit), chans, columns), F32)
-            keep, send = call(halve_body, [half, half], [], (keep, got))
+        half = shape((groups // (4 * bit), chans, columns), F32)
+        keep, send = call(halve_body, [half, half], [], (keep, got))
         bit *= 2
+    step = bits[0]
+    held = [
+        keep,
+        lax.ppermute(keep, ("gx", "gy"), [(i, i ^ step) for i in range(count)]),
+        across(send, bit, sizes),
+        lax.ppermute(send, ALL, [(i, i ^ (step * groups) ^ bit) for i in range(count * groups)]),
+    ]
 
     pieces = call(
         bind(outputs_body, sizes),
@@ -638,13 +649,9 @@
     )
 
     own = shape((1, chans, columns), F32)
-    (total,) = call(sum_body, [own], [], (keep, got))
-    count = sizes["gx"] * sizes["gy"]
-    bits = [1 << n for n in range((count - 1).bit_length())]
-    bits.remove(sizes["gy"])
-    bits.reverse()
-    for bit in bits[:-1]:
-        got = lax.ppermute(total, ("gx", "gy"), [(i, i ^ bit) for i in range(count)])
+    (total,) = call(sum_body, [own], [], held)
+    for step in bits[1:-1]:
+        got = lax.ppermute(total, ("gx", "gy"), [(i, i ^ step) for i in range(count)])
         (total,) = call(sum_body, [own], [], (total, got))
     got = [
         lax.ppermute(total, ("gx", "gy"), [(i, i ^ step) for i in range(count)])

time: 51.9 us -> 52.6 us (1.013)
  starting transfers between devices: 22.5 us -> 24 us
  waiting for transfers between devices: 19.5 us -> 18.7 us
    ppermute x1 -> x2, starting transfers between devices: 0.54 us -> 3.06 us  [the longest x1 2.45 us: body(): lax.ppermute(send, ALL, [(i, i ^ step * groups ^ bit) for i in range(coun...]
    ppermute x8, waiting for transfers between devices: 8.59 us -> 7.21 us  [across(): lax.ppermute(value, 'af', [(i, i ^ step) for i in range(sizes['af'])])]
    ppermute x8, starting transfers between devices: 13.3 us -> 12.2 us  [across(): lax.ppermute(value, 'af', [(i, i ^ step) for i in range(sizes['af'])])]
    ppermute x1 -> x2, waiting for transfers between devices: 3.33 us -> 3.9 us  [the longest x1 3.9 us: body(): lax.ppermute(send, ALL, [(i, i ^ step * groups ^ bit) for i in range(coun...]
    pallas_call x12 -> x11, Pallas kernels: 9.04 us -> 9.04 us  [call(): pl.pallas_call(body, out_shape=tuple(outs), in_specs=specs or [pl.BlockSp...]
  transfers between devices with their start and end apart: 20 -> 21, of which waited for: 10 -> 9; matrix products, arithmetic and copies ran while one was open for 0% -> 0% of each run, Pallas kernels for 9% -> 9%
where the time goes in v3:
time: 52.6 us; the launch traced here: 52.5 us
  starting transfers between devices  24 us (46%)
  waiting for transfers between devices  18.7 us (36%)
  Pallas kernels  9.04 us (17%)
  between operations  0.75 us (1%)
    ppermute x8, starting transfers between devices, across(): lax.ppermute(value, 'af', [(i, i ^ step) for i in range(sizes['af'])])  12.2 us
    pallas_call x11, Pallas kernels, call(): pl.pallas_call(body, out_shape=tuple(outs), in_specs=specs or [pl.BlockSp...  9.04 us
    ppermute x8, waiting for transfers between devices, across(): lax.ppermute(value, 'af', [(i, i ^ step) for i in range(sizes['af'])])  7.21 us
    ppermute x1, waiting for transfers between devices, body(): lax.ppermute(send, ALL, [(i, i ^ step * groups ^ bit) for i in range(coun...  3.9 us
    ppermute x3, waiting for transfers between devices, body(): lax.ppermute(total, ('gx', 'gy'), [(i, i ^ step) for i in range(count)])  3.32 us
    ppermute x1, starting transfers between devices, body(): lax.ppermute(send, ALL, [(i, i ^ step * groups ^ bit) for i in range(coun...  2.45 us
    ppermute x3, starting transfers between devices, body(): lax.ppermute(total, ('gx', 'gy'), [(i, i ^ step) for i in range(count)])  2.2 us
    ppermute x2, starting transfers between devices, body(): corners = (lax.ppermute(c_one, 'gx', near), lax.ppermute(c_two, 'gx', wrap))  1.66 us
  transfers between devices with their start and end apart: 21, of which 9 were waited for; matrix products, arithmetic and copies ran while one was open for 0% of the time, Pallas kernels for 9%

profile of v3, /device:TPU:0, one launch (start us, length us, event | category | flops | bytes accessed | tf_op | source)
XLA Modules:
  0.0 52.5 jit_solution(14330994268515900280)
XLA Ops:
  0.6 1.3 %shard_map.92 = (bf16[39,8,128]{2,1,0:T(8,128)(2,1)S(1)}, bf16[39,8,128]{2,1,0:T(8,128)(2,1)S(1)}, bf16[39,8,128]{2,1,0:T(8,128)(2,1)S(1)}, bf16[39,8,128]{2,1,0:T(8,128)(2,1)S(1)}) custom-call(bf16[8,4,16,128]{3,2,1,0:T(8,128)(2,1)} %vol_hbm.1, bf16[8,4,16,128]{3,2,1,0:T(8,128)(2,1)} %cot_hbm.1, bf16[27,8,32]{2,1,0:T(8,128)(2,1)} %bitcast.14, ...), custom_call_target="tpu_custom_call" | custom-call | bytes 609312 | tf_op jit(solution)/shard_map/pallas_call | solution.py:497
  1.9 3.1 %collective-permute-start = (bf16[39,8,128]{2,1,0:T(8,128)(2,1)S(1)}, bf16[39,8,128]{2,1,0:T(8,128)(2,1)S(1)}, u32[]{:S(2)}, u32[]{:S(2)}) collective-permute-start(bf16[39,8,128]{2,1,0:T(8,128)(2,1)S(1)} %get-tuple-element.45), channel_id=1, source_target_pairs={{0,1},{1,0},{2,3},{3,2},{4,5},{5,4},{6,7},{7,6},{8,9},{9,8},{10,11... | collective-permute-start | bytes 239624 | tf_op jit(solution)/shard_map/ppermute | solution.py:509
  5.0 2.6 %collective-permute-start.1 = (bf16[39,8,128]{2,1,0:T(8,128)(2,1)S(1)}, bf16[39,8,128]{2,1,0:T(8,128)(2,1)S(1)}, u32[]{:S(2)}, u32[]{:S(2)}) collective-permute-start(bf16[39,8,128]{2,1,0:T(8,128)(2,1)S(1)} %get-tuple-element.46), channel_id=1, source_target_pairs={{0,2},{1,3},{2,0},{3,1},{4,6},{5,7},{6,4},{7,5},{8,10},{9,11},{10,... | collective-permute-start | bytes 239624 | tf_op jit(solution)/shard_map/ppermute | solution.py:509
  7.6 6.4 %collective-permute-done.1.refs_2_ = bf16[39,8,128]{2,1,0:T(8,128)(2,1)S(1)} collective-permute-done((bf16[39,8,128]{2,1,0:T(8,128)(2,1)S(1)}, bf16[39,8,128]{2,1,0:T(8,128)(2,1)S(1)}, u32[]{:S(2)}, u32[]{:S(2)}) %collective-permute-start.1) | collective-permute-done | bytes 79904 | tf_op jit(solution)/shard_map/ppermute | solution.py:509
  14.3 1.5 %collective-permute-start.3 = (bf16[2,4,2,32,128]{4,3,2,1,0:T(8,128)(2,1)S(1)}, bf16[2,4,2,32,128]{4,3,2,1,0:T(8,128)(2,1)S(1)}, u32[]{:S(2)}, u32[]{:S(2)}) collective-permute-start(bf16[2,4,2,32,128]{4,3,2,1,0:T(8,128)(2,1)S(1)} %get-tuple-element.49), channel_id=1, source_target_pairs={{0,1},{1,0},{2,3},{3,2},{7,6},{6,7},{5,4},{4,5},{8,9},{9,8},{10,11... | collective-permute-start | bytes 393224 | tf_op jit(solution)/shard_map/ppermute | solution.py:584
  15.7 1.5 %collective-permute-start.4 = (bf16[2,4,2,32,128]{4,3,2,1,0:T(8,128)(2,1)S(1)}, bf16[2,4,2,32,128]{4,3,2,1,0:T(8,128)(2,1)S(1)}, u32[]{:S(2)}, u32[]{:S(2)}) collective-permute-start(bf16[2,4,2,32,128]{4,3,2,1,0:T(8,128)(2,1)S(1)} %get-tuple-element.50), channel_id=1, source_target_pairs={{0,4},{1,2},{2,1},{3,7},{7,3},{6,5},{5,6},{4,0},{8,12},{9,10},{10,... | collective-permute-start | bytes 393224 | tf_op jit(solution)/shard_map/ppermute | solution.py:585
  17.2 1.6 %collective-permute-start.6 = (bf16[2,2,4,32,128]{4,3,2,1,0:T(8,128)(2,1)S(1)}, bf16[2,2,4,32,128]{4,3,2,1,0:T(8,128)(2,1)S(1)}, u32[]{:S(2)}, u32[]{:S(2)}) collective-permute-start(bf16[2,2,4,32,128]{4,3,2,1,0:T(8,128)(2,1)S(1)} %get-tuple-element.52), channel_id=1, source_target_pairs={{0,24},{8,16},{16,8},{24,0},{1,25},{9,17},{17,9},{25,1},{2,26},{10... | collective-permute-start | bytes 393224 | tf_op jit(solution)/shard_map/ppermute | solution.py:587
  19.3 1.4 %collective-permute-done.4.yb = bf16[2,4,2,32,128]{4,3,2,1,0:T(8,128)(2,1)S(1)} collective-permute-done((bf16[2,4,2,32,128]{4,3,2,1,0:T(8,128)(2,1)S(1)}, bf16[2,4,2,32,128]{4,3,2,1,0:T(8,128)(2,1)S(1)}, u32[]{:S(2)}, u32[]{:S(2)}) %collective-permute-start.4) | collective-permute-done | bytes 131104 | tf_op jit(solution)/shard_map/ppermute | solution.py:585
  20.8 1.6 %collective-permute-start.9 = (bf16[2,2,4,32,128]{4,3,2,1,0:T(8,128)(2,1)S(1)}, bf16[2,2,4,32,128]{4,3,2,1,0:T(8,128)(2,1)S(1)}, u32[]{:S(2)}, u32[]{:S(2)}) collective-permute-start(bf16[2,2,4,32,128]{4,3,2,1,0:T(8,128)(2,1)S(1)} %get-tuple-element.59), channel_id=1, source_target_pairs={{0,24},{8,16},{16,8},{24,0},{1,25},{9,17},{17,9},{25,1},{2,26},{10... | collective-permute-start | bytes 393224 | tf_op jit(solution)/shard_map/ppermute | solution.py:592
  22.5 1.2 %collective-permute-done.7.other_ref = bf16[32,896]{1,0:T(8,128)(2,1)S(1)} collective-permute-done((bf16[32,896]{1,0:T(8,128)(2,1)S(1)}, bf16[32,896]{1,0:T(8,128)(2,1)S(1)}, u32[]{:S(2)}, u32[]{:S(2)}) %collective-permute-start.7) | collective-permute-done | bytes 57376 | tf_op jit(solution)/shard_map/ppermute | solution.py:588
  24.0 3.1 %shard_map.95 = (bf16[8,8,96,128]{3,2,1,0:T(8,128)(2,1)S(1)}, bf16[8,8,96,128]{3,2,1,0:T(8,128)(2,1)S(1)}, bf16[6,6,96,128]{3,2,1,0:T(8,128)(2,1)S(1)}, bf16[6,6...) custom-call(bf16[2,4,4,32,128]{4,3,2,1,0:T(8,128)(2,1)S(1)} %get-tuple-element.48.core, ...), custom_call_target="tpu_custom_call" | custom-call | flops 264241152 | bytes 6340608 | tf_op jit(solution)/shard_map/pallas_call | solution.py:497
  27.1 1.9 %shard_map.97 = (bf16[4,4,96,128]{3,2,1,0:T(8,128)(2,1)S(1)}, bf16[4,4,96,128]{3,2,1,0:T(8,128)(2,1)S(1)}, f32[32,896]{1,0:T(8,128)S(1)}, f32[32,896]{1,0:T(8,128)S(1)}) custom-call(bf16[2,2,4,32,128]{4,3,2,1,0:T(8,128)(2,1)S(1)} %collective-permute-done.8.ca, bf16[2,2,4,32,128]{4,3,2,1,0:T(8,128)(2,1)S(1)} %collective-permute-done.9.cb, ...), custom_call_target="tpu_custom_call" | custom-call | flops 499122176 | bytes 6832128 | tf_op jit(solution)/shard_map/pallas_call | solution.py:497
  29.2 1.2 %collective-permute-done.13.got_ref = f32[32,896]{1,0:T(8,128)S(1)} collective-permute-done((f32[32,896]{1,0:T(8,128)S(1)}, f32[32,896]{1,0:T(8,128)S(1)}, u32[]{:S(2)}, u32[]{:S(2)}) %collective-permute-start.13) | collective-permute-done | bytes 114720 | tf_op jit(solution)/shard_map/ppermute | solution.py:618
  31.1 1.3 %shard_map.98 = (bf16[4,2,4,8,128]{4,3,2,1,0:T(8,128)(2,1)S(1)}, bf16[4,2,4,8,128]{4,3,2,1,0:T(8,128)(2,1)S(1)}, bf16[4,2,4,8,128]{4,3,2,1,0:T(8,128)(2,1)S(1)}, bf16[4,2,4,8,128]{4,3,2,1,0:T(8,128)(2,1)S(1)}) custom-call(bf16[6,6,96,128]{3,2,1,0:T(8,128)(2,1)S(1)} %get-tuple-element.56.hid_e, bf16[6,6,96,128]{3,2,1,0:T(8,128)(2,1)S(1)} %get-tuple-element.57.pre_e, ...), custom_call_target="tpu_custom_call" | custom-call | flops 234881024 | bytes 2932736 | tf_op jit(solution)/shard_map/pallas_call | solution.py:497
  32.4 1.5 %collective-permute-start.10 = (bf16[4,2,4,8,128]{4,3,2,1,0:T(8,128)(2,1)S(1)}, bf16[4,2,4,8,128]{4,3,2,1,0:T(8,128)(2,1)S(1)}, u32[]{:S(2)}, u32[]{:S(2)}) collective-permute-start(bf16[4,2,4,8,128]{4,3,2,1,0:T(8,128)(2,1)S(1)} %get-tuple-element.69), channel_id=1, source_target_pairs={{0,1},{1,0},{2,3},{3,2},{4,5},{5,4},{6,7},{7,6},{8,9},{9,8},{10,11... | collective-permute-start | bytes 196616 | tf_op jit(solution)/shard_map/ppermute | solution.py:509
  35.3 1.6 %collective-permute-start.11 = (bf16[4,2,4,8,128]{4,3,2,1,0:T(8,128)(2,1)S(1)}, bf16[4,2,4,8,128]{4,3,2,1,0:T(8,128)(2,1)S(1)}, u32[]{:S(2)}, u32[]{:S(2)}) collective-permute-start(bf16[4,2,4,8,128]{4,3,2,1,0:T(8,128)(2,1)S(1)} %get-tuple-element.70), channel_id=1, source_target_pairs={{0,2},{1,3},{2,0},{3,1},{4,6},{5,7},{6,4},{7,5},{8,10},{9,11},{10,... | collective-permute-start | bytes 196616 | tf_op jit(solution)/shard_map/ppermute | solution.py:509
  36.9 1.3 %collective-permute-start.12 = (bf16[4,2,4,8,128]{4,3,2,1,0:T(8,128)(2,1)S(1)}, bf16[4,2,4,8,128]{4,3,2,1,0:T(8,128)(2,1)S(1)}, u32[]{:S(2)}, u32[]{:S(2)}) collective-permute-start(bf16[4,2,4,8,128]{4,3,2,1,0:T(8,128)(2,1)S(1)} %get-tuple-element.71), channel_id=1, source_target_pairs={{0,3},{1,2},{2,1},{3,0},{4,7},{5,6},{6,5},{7,4},{8,11},{9,10},{10,... | collective-permute-start | bytes 196616 | tf_op jit(solution)/shard_map/ppermute | solution.py:509
  38.3 2.5 %collective-permute-start.17 = (f32[1,8,896]{2,1,0:T(8,128)S(1)}, f32[1,8,896]{2,1,0:T(8,128)S(1)}, u32[]{:S(2)}, u32[]{:S(2)}) collective-permute-start(f32[1,8,896]{2,1,0:T(8,128)S(1)} %get-tuple-element.77), channel_id=1, source_target_pairs={{0,18},{1,19},{2,16},{3,17},{4,22},{5,23},{6,20},{7,21},{8,26},{9,... | collective-permute-start | bytes 86024 | tf_op jit(solution)/shard_map/ppermute | solution.py:640
  40.7 1.4 %collective-permute-start.16 = (f32[1,8,896]{2,1,0:T(8,128)S(1)}, f32[1,8,896]{2,1,0:T(8,128)S(1)}, u32[]{:S(2)}, u32[]{:S(2)}) collective-permute-start(f32[1,8,896]{2,1,0:T(8,128)S(1)} %get-tuple-element.77), channel_id=1, source_target_pairs={{0,2},{1,3},{2,0},{3,1},{4,6},{5,7},{6,4},{7,5},{8,10},{9,11},{10,... | collective-permute-start | bytes 86024 | tf_op jit(solution)/shard_map/ppermute | solution.py:509
  42.1 3.9 %collective-permute-done.17.refs_3_ = f32[1,8,896]{2,1,0:T(8,128)S(1)} collective-permute-done((f32[1,8,896]{2,1,0:T(8,128)S(1)}, f32[1,8,896]{2,1,0:T(8,128)S(1)}, u32[]{:S(2)}, u32[]{:S(2)}) %collective-permute-start.17) | collective-permute-done | bytes 28704 | tf_op jit(solution)/shard_map/ppermute | solution.py:640
  46.1 1.6 %collective-permute-start.19 = (f32[1,8,896]{2,1,0:T(8,128)S(1)}, f32[1,8,896]{2,1,0:T(8,128)S(1)}, u32[]{:S(2)}, u32[]{:S(2)}) collective-permute-start(f32[1,8,896]{2,1,0:T(8,128)S(1)} %shard_map.101.refs_4_), channel_id=1, source_target_pairs={{0,12},{4,8},{8,4},{12,0},{16,28},{20,24},{24,20},{28,16},{1,13},{... | collective-permute-start | bytes 86024 | tf_op jit(solution)/shard_map/ppermute | solution.py:657
  48.3 1.2 %collective-permute-done.19.refs_6_ = f32[1,8,896]{2,1,0:T(8,128)S(1)} collective-permute-done((f32[1,8,896]{2,1,0:T(8,128)S(1)}, f32[1,8,896]{2,1,0:T(8,128)S(1)}, u32[]{:S(2)}, u32[]{:S(2)}) %collective-permute-start.19) | collective-permute-done | bytes 28704 | tf_op jit(solution)/shard_map/ppermute | solution.py:657
  49.5 2.1 %collective-permute-done.18.refs_5_ = f32[1,8,896]{2,1,0:T(8,128)S(1)} collective-permute-done((f32[1,8,896]{2,1,0:T(8,128)S(1)}, f32[1,8,896]{2,1,0:T(8,128)S(1)}, u32[]{:S(2)}, u32[]{:S(2)}) %collective-permute-start.18) | collective-permute-done | bytes 28704 | tf_op jit(solution)/shard_map/ppermute | solution.py:657
  51.6 0.9 %shard_map.102 = (bf16[8,4,16,128]{3,2,1,0:T(8,128)(2,1)}, bf16[8,4,16,128]{3,2,1,0:T(8,128)(2,1)}, f32[27,8,32]{2,1,0:T(8,128)}, f32[27,8,32]{2,1,0:T(8,128)}, f32[1,8]{1,0:T(1,128)}) custom-call(bf16[4,2,4,8,128]{4,3,2,1,0:T(8,128)(2,1)S(1)} %get-tuple-element.68.refs_0_, bf16[4,2,4,8,128]{4,3,2,1,0:T(8,128)(2,1)S(1)} %collective-permute-done.10.refs_1_, ...), custom_call_target="tpu_custom_call" | custom-call | bytes 694304 | tf_op jit(solution)/shard_map/pallas_call | solution.py:497
  (29 shorter events, 4.1 us)
Async XLA Ops:
  1.9 5.7 %collective-permute-start = (bf16[39,8,128]{2,1,0:T(8,128)(2,1)S(1)}, bf16[39,8,128]{2,1,0:T(8,128)(2,1)S(1)}, u32[]{:S(2)}, u32[]{:S(2)}) collective-permute-start(bf16[39,8,128]{2,1,0:T(8,128)(2,1)S(1)} %get-tuple-element.45), channel_id=1, source_target_pairs={{0,1},{1,0},{2,3},{3,2},{4,5},{5,4},{6,7},{7,6},{8,9},{9,8},{10,11... | collective-permute-start | bytes 239624 | tf_op jit(solution)/shard_map/ppermute | solution.py:509
  5.0 9.0 %collective-permute-start.1 = (bf16[39,8,128]{2,1,0:T(8,128)(2,1)S(1)}, bf16[39,8,128]{2,1,0:T(8,128)(2,1)S(1)}, u32[]{:S(2)}, u32[]{:S(2)}) collective-permute-start(bf16[39,8,128]{2,1,0:T(8,128)(2,1)S(1)} %get-tuple-element.46), channel_id=1, source_target_pairs={{0,2},{1,3},{2,0},{3,1},{4,6},{5,7},{6,4},{7,5},{8,10},{9,11},{10,... | collective-permute-start | bytes 239624 | tf_op jit(solution)/shard_map/ppermute | solution.py:509
  7.6 6.5 %collective-permute-start.2 = (bf16[39,8,128]{2,1,0:T(8,128)(2,1)S(1)}, bf16[39,8,128]{2,1,0:T(8,128)(2,1)S(1)}, u32[]{:S(2)}, u32[]{:S(2)}) collective-permute-start(bf16[39,8,128]{2,1,0:T(8,128)(2,1)S(1)} %get-tuple-element.47), channel_id=1, source_target_pairs={{0,3},{1,2},{2,1},{3,0},{4,7},{5,6},{6,5},{7,4},{8,11},{9,10},{10,... | collective-permute-start | bytes 239624 | tf_op jit(solution)/shard_map/ppermute | solution.py:509
  14.3 5.0 %collective-permute-start.3 = (bf16[2,4,2,32,128]{4,3,2,1,0:T(8,128)(2,1)S(1)}, bf16[2,4,2,32,128]{4,3,2,1,0:T(8,128)(2,1)S(1)}, u32[]{:S(2)}, u32[]{:S(2)}) collective-permute-start(bf16[2,4,2,32,128]{4,3,2,1,0:T(8,128)(2,1)S(1)} %get-tuple-element.49), channel_id=1, source_target_pairs={{0,1},{1,0},{2,3},{3,2},{7,6},{6,7},{5,4},{4,5},{8,9},{9,8},{10,11... | collective-permute-start | bytes 393224 | tf_op jit(solution)/shard_map/ppermute | solution.py:584
  15.7 5.0 %collective-permute-start.4 = (bf16[2,4,2,32,128]{4,3,2,1,0:T(8,128)(2,1)S(1)}, bf16[2,4,2,32,128]{4,3,2,1,0:T(8,128)(2,1)S(1)}, u32[]{:S(2)}, u32[]{:S(2)}) collective-permute-start(bf16[2,4,2,32,128]{4,3,2,1,0:T(8,128)(2,1)S(1)} %get-tuple-element.50), channel_id=1, source_target_pairs={{0,4},{1,2},{2,1},{3,7},{7,3},{6,5},{5,6},{4,0},{8,12},{9,10},{10,... | collective-permute-start | bytes 393224 | tf_op jit(solution)/shard_map/ppermute | solution.py:585
  17.2 6.8 %collective-permute-start.5 = (bf16[2,2,4,32,128]{4,3,2,1,0:T(8,128)(2,1)S(1)}, bf16[2,2,4,32,128]{4,3,2,1,0:T(8,128)(2,1)S(1)}, u32[]{:S(2)}, u32[]{:S(2)}) collective-permute-start(bf16[2,2,4,32,128]{4,3,2,1,0:T(8,128)(2,1)S(1)} %get-tuple-element.51), channel_id=1, source_target_pairs={{0,8},{8,0},{16,24},{24,16},{1,9},{9,1},{17,25},{25,17},{2,10},{10... | collective-permute-start | bytes 393224 | tf_op jit(solution)/shard_map/ppermute | solution.py:587
  17.2 6.8 %collective-permute-start.6 = (bf16[2,2,4,32,128]{4,3,2,1,0:T(8,128)(2,1)S(1)}, bf16[2,2,4,32,128]{4,3,2,1,0:T(8,128)(2,1)S(1)}, u32[]{:S(2)}, u32[]{:S(2)}) collective-permute-start(bf16[2,2,4,32,128]{4,3,2,1,0:T(8,128)(2,1)S(1)} %get-tuple-element.52), channel_id=1, source_target_pairs={{0,24},{8,16},{16,8},{24,0},{1,25},{9,17},{17,9},{25,1},{2,26},{10... | collective-permute-start | bytes 393224 | tf_op jit(solution)/shard_map/ppermute | solution.py:587
  20.7 6.3 %collective-permute-start.8 = (bf16[2,2,4,32,128]{4,3,2,1,0:T(8,128)(2,1)S(1)}, bf16[2,2,4,32,128]{4,3,2,1,0:T(8,128)(2,1)S(1)}, u32[]{:S(2)}, u32[]{:S(2)}) collective-permute-start(bf16[2,2,4,32,128]{4,3,2,1,0:T(8,128)(2,1)S(1)} %get-tuple-element.58), channel_id=1, source_target_pairs={{0,8},{8,0},{16,24},{24,16},{1,9},{9,1},{17,25},{25,17},{2,10},{10... | collective-permute-start | bytes 393224 | tf_op jit(solution)/shard_map/ppermute | solution.py:592
  20.8 6.3 %collective-permute-start.9 = (bf16[2,2,4,32,128]{4,3,2,1,0:T(8,128)(2,1)S(1)}, bf16[2,2,4,32,128]{4,3,2,1,0:T(8,128)(2,1)S(1)}, u32[]{:S(2)}, u32[]{:S(2)}) collective-permute-start(bf16[2,2,4,32,128]{4,3,2,1,0:T(8,128)(2,1)S(1)} %get-tuple-element.59), channel_id=1, source_target_pairs={{0,24},{8,16},{16,8},{24,0},{1,25},{9,17},{17,9},{25,1},{2,26},{10... | collective-permute-start | bytes 393224 | tf_op jit(solution)/shard_map/ppermute | solution.py:592
  22.4 1.2 %collective-permute-start.7 = (bf16[32,896]{1,0:T(8,128)(2,1)S(1)}, bf16[32,896]{1,0:T(8,128)(2,1)S(1)}, u32[]{:S(2)}, u32[]{:S(2)}) collective-permute-start(bf16[32,896]{1,0:T(8,128)(2,1)S(1)} %get-tuple-element.53.mine_ref), channel_id=1, source_target_pairs={{0,8},{8,0},{16,24},{24,16},{1,9},{9,1},{17,25},{25,17},{2,10},{10... | collective-permute-start | bytes 172040 | tf_op jit(solution)/shard_map/ppermute | solution.py:588
  29.0 1.4 %collective-permute-start.13 = (f32[32,896]{1,0:T(8,128)S(1)}, f32[32,896]{1,0:T(8,128)S(1)}, u32[]{:S(2)}, u32[]{:S(2)}) collective-permute-start(f32[32,896]{1,0:T(8,128)S(1)} %get-tuple-element.73), channel_id=1, source_target_pairs={{0,8},{8,0},{16,24},{24,16},{1,9},{9,1},{17,25},{25,17},{2,10},{10... | collective-permute-start | bytes 344072 | tf_op jit(solution)/shard_map/ppermute | solution.py:618
  30.4 4.2 %collective-permute-start.14 = (f32[2,8,896]{2,1,0:T(8,128)S(1)}, f32[2,8,896]{2,1,0:T(8,128)S(1)}, u32[]{:S(2)}, u32[]{:S(2)}) collective-permute-start(f32[2,8,896]{2,1,0:T(8,128)S(1)} %get-tuple-element.75), channel_id=1, source_target_pairs={{0,1},{1,0},{2,3},{3,2},{4,5},{5,4},{6,7},{7,6},{8,9},{9,8},{10,11... | collective-permute-start | bytes 172040 | tf_op jit(solution)/shard_map/ppermute | solution.py:509
  32.4 15.3 %collective-permute-start.10 = (bf16[4,2,4,8,128]{4,3,2,1,0:T(8,128)(2,1)S(1)}, bf16[4,2,4,8,128]{4,3,2,1,0:T(8,128)(2,1)S(1)}, u32[]{:S(2)}, u32[]{:S(2)}) collective-permute-start(bf16[4,2,4,8,128]{4,3,2,1,0:T(8,128)(2,1)S(1)} %get-tuple-element.69), channel_id=1, source_target_pairs={{0,1},{1,0},{2,3},{3,2},{4,5},{5,4},{6,7},{7,6},{8,9},{9,8},{10,11... | collective-permute-start | bytes 196616 | tf_op jit(solution)/shard_map/ppermute | solution.py:509
  34.7 6.0 %collective-permute-start.15 = (f32[1,8,896]{2,1,0:T(8,128)S(1)}, f32[1,8,896]{2,1,0:T(8,128)S(1)}, u32[]{:S(2)}, u32[]{:S(2)}) collective-permute-start(f32[1,8,896]{2,1,0:T(8,128)S(1)} %get-tuple-element.76.refs_0_), channel_id=1, source_target_pairs={{0,16},{4,20},{8,24},{12,28},{16,0},{20,4},{24,8},{28,12},{1,17},{... | collective-permute-start | bytes 86024 | tf_op jit(solution)/shard_map/ppermute | solution.py:638
  35.3 13.0 %collective-permute-start.11 = (bf16[4,2,4,8,128]{4,3,2,1,0:T(8,128)(2,1)S(1)}, bf16[4,2,4,8,128]{4,3,2,1,0:T(8,128)(2,1)S(1)}, u32[]{:S(2)}, u32[]{:S(2)}) collective-permute-start(bf16[4,2,4,8,128]{4,3,2,1,0:T(8,128)(2,1)S(1)} %get-tuple-element.70), channel_id=1, source_target_pairs={{0,2},{1,3},{2,0},{3,1},{4,6},{5,7},{6,4},{7,5},{8,10},{9,11},{10,... | collective-permute-start | bytes 196616 | tf_op jit(solution)/shard_map/ppermute | solution.py:509
  36.9 11.3 %collective-permute-start.12 = (bf16[4,2,4,8,128]{4,3,2,1,0:T(8,128)(2,1)S(1)}, bf16[4,2,4,8,128]{4,3,2,1,0:T(8,128)(2,1)S(1)}, u32[]{:S(2)}, u32[]{:S(2)}) collective-permute-start(bf16[4,2,4,8,128]{4,3,2,1,0:T(8,128)(2,1)S(1)} %get-tuple-element.71), channel_id=1, source_target_pairs={{0,3},{1,2},{2,1},{3,0},{4,7},{5,6},{6,5},{7,4},{8,11},{9,10},{10,... | collective-permute-start | bytes 196616 | tf_op jit(solution)/shard_map/ppermute | solution.py:509
  38.3 7.8 %collective-permute-start.17 = (f32[1,8,896]{2,1,0:T(8,128)S(1)}, f32[1,8,896]{2,1,0:T(8,128)S(1)}, u32[]{:S(2)}, u32[]{:S(2)}) collective-permute-start(f32[1,8,896]{2,1,0:T(8,128)S(1)} %get-tuple-element.77), channel_id=1, source_target_pairs={{0,18},{1,19},{2,16},{3,17},{4,22},{5,23},{6,20},{7,21},{8,26},{9,... | collective-permute-start | bytes 86024 | tf_op jit(solution)/shard_map/ppermute | solution.py:640
  40.7 5.3 %collective-permute-start.16 = (f32[1,8,896]{2,1,0:T(8,128)S(1)}, f32[1,8,896]{2,1,0:T(8,128)S(1)}, u32[]{:S(2)}, u32[]{:S(2)}) collective-permute-start(f32[1,8,896]{2,1,0:T(8,128)S(1)} %get-tuple-element.77), channel_id=1, source_target_pairs={{0,2},{1,3},{2,0},{3,1},{4,6},{5,7},{6,4},{7,5},{8,10},{9,11},{10,... | collective-permute-start | bytes 86024 | tf_op jit(solution)/shard_map/ppermute | solution.py:509
  46.0 2.2 %collective-permute-start.20 = (f32[1,8,896]{2,1,0:T(8,128)S(1)}, f32[1,8,896]{2,1,0:T(8,128)S(1)}, u32[]{:S(2)}, u32[]{:S(2)}) collective-permute-start(f32[1,8,896]{2,1,0:T(8,128)S(1)} %shard_map.101.refs_4_), channel_id=1, source_target_pairs={{0,8},{4,12},{8,0},{12,4},{16,24},{20,28},{24,16},{28,20},{1,9},{5... | collective-permute-start | bytes 86024 | tf_op jit(solution)/shard_map/ppermute | solution.py:657
  46.1 3.4 %collective-permute-start.19 = (f32[1,8,896]{2,1,0:T(8,128)S(1)}, f32[1,8,896]{2,1,0:T(8,128)S(1)}, u32[]{:S(2)}, u32[]{:S(2)}) collective-permute-start(f32[1,8,896]{2,1,0:T(8,128)S(1)} %shard_map.101.refs_4_), channel_id=1, source_target_pairs={{0,12},{4,8},{8,4},{12,0},{16,28},{20,24},{24,20},{28,16},{1,13},{... | collective-permute-start | bytes 86024 | tf_op jit(solution)/shard_map/ppermute | solution.py:657
  47.7 3.9 %collective-permute-start.18 = (f32[1,8,896]{2,1,0:T(8,128)S(1)}, f32[1,8,896]{2,1,0:T(8,128)S(1)}, u32[]{:S(2)}, u32[]{:S(2)}) collective-permute-start(f32[1,8,896]{2,1,0:T(8,128)S(1)} %shard_map.101.refs_4_), channel_id=1, source_target_pairs={{0,4},{4,0},{8,12},{12,8},{16,20},{20,16},{24,28},{28,24},{1,5},{5... | collective-permute-start | bytes 86024 | tf_op jit(solution)/shard_map/ppermute | solution.py:657
